TPU v7x, 256 devices: a whole 4x4x8 slice. The times are simulated.
256 devices in a mesh: emb: 32 (over z_hi, y, core), wide: 8 (over x, z_lo).
Axes of the slice: x: 4, y: 4, z: 8 (z_hi: 4, z_lo: 2; z = z_hi * 2 + z_lo), core: 2. Of those that a mesh axis runs over, the one named last changes fastest.
Arguments:
- tables: bfloat16 [512, 512, 256], P('emb'), may hold values from -3 to 3
- bag_ids: int32 [8, 128, 512, 4], P('wide', None, 'emb'), may hold values from 0 to 511
- bag_lengths: int32 [8, 128, 512], P('wide', None, 'emb'), may hold values from 1 to 4
- slot_field: int32 [512], replicated, may hold values from 0 to 511, each once
- proj_y: bfloat16 [512, 256], replicated, may hold values from -0.25 to 0.25
- proj_p: bfloat16 [128, 512], replicated, may hold values from -0.25 to 0.25
- linear_w: bfloat16 [384, 512], replicated, may hold values from -0.25 to 0.25
- fm_gain: float32 [256], replicated, may hold values from 0.5 to 1.5
- w_up: bfloat16 [8192, 256], P('wide'), may hold values from -0.375 to 0.375
- w_down: bfloat16 [8192, 256], P('wide'), may hold values from -0.0625 to 0.0625
- out_gain: float32 [256], replicated, may hold values from 0.5 to 1.5
- cotangent: bfloat16 [8, 128, 512, 256], P('wide', 'emb'), may hold values from -6 to 6
Outputs:
- layer_out: bfloat16 [8, 128, 512, 256], P('wide', 'emb')
- pooled_grad: bfloat16 [8, 128, 512, 256], P('wide', None, 'emb')
- grad_up: float32 [8192, 256], P('wide')
- grad_down: float32 [8192, 256], P('wide')
Inputs may be any that keep to these rules, and one draw needn't show every extreme that they name: `bag_ids`: each id indexes a bucket of the table of its slot. `slot_field`: each field appears in exactly one slot.
All inputs are finite; a program needn't handle non-finite values.
Results may differ from a plain program's by a relative error of at most 0.008.
Values may be sent and summed in bfloat16 or wider, within the bound.
A program may use at most 128 MiB of HBM per device.

v0:
```python
import jax
import jax.numpy as jnp
from jax import lax
from jax.sharding import PartitionSpec as P

NF = 128


norm_eps = 1e-05


def layer_norm(values):
    centre = jnp.mean(values, axis=-1, keepdims=True)
    shifted = values - centre
    scale = lax.rsqrt(jnp.mean(shifted * shifted, axis=-1, keepdims=True) + norm_eps)
    return (shifted * scale, scale)


def norm_back(unit, scale, gain, upstream):
    scaled = upstream * gain
    return scale * (
        scaled
        - jnp.mean(scaled, axis=-1, keepdims=True)
        - unit * jnp.mean(scaled * unit, axis=-1, keepdims=True)
    )


def silu_back(values):
    sigma = jax.nn.sigmoid(values)
    return sigma * (1.0 + values * (1.0 - sigma))


def pool_bags(tables, ids, lengths):
    slots_here = tables.shape[0]
    bucket_count = tables.shape[1]
    flat_ids = ids + (jnp.arange(slots_here, dtype=jnp.int32) * bucket_count)[None, :, None]
    gathered = jnp.take(tables.reshape(slots_here * bucket_count, -1), flat_ids, axis=0)
    live = (jnp.arange(ids.shape[2], dtype=jnp.int32)[None, None, :] < lengths[:, :, None]).astype(
        jnp.bfloat16
    )
    return jnp.einsum("gfj,gfje->gfe", live, gathered, preferred_element_type=jnp.float32).astype(
        jnp.bfloat16
    )


def body(
    tables,
    bag_ids,
    bag_lengths,
    slot_field,
    proj_y,
    proj_p,
    linear_w,
    fm_gain,
    w_up,
    w_down,
    out_gain,
    cotangent,
):
    pooled = pool_bags(tables, bag_ids[0], bag_lengths[0])[None]
    received = lax.all_to_all(pooled, "emb", split_axis=1, concat_axis=2, tiled=True)
    slot_embeds = received[0]
    embeds = jnp.zeros_like(slot_embeds).at[:, slot_field].set(slot_embeds)
    samples = embeds.shape[0]
    crossed = jnp.einsum("bfe,fk->bek", embeds, proj_y, preferred_element_type=jnp.float32).astype(
        jnp.bfloat16
    )
    mixing = jnp.einsum("nf,bfe->bne", proj_p, embeds, preferred_element_type=jnp.float32).astype(
        jnp.bfloat16
    )
    inter = jnp.einsum("bne,bek->bnk", mixing, crossed, preferred_element_type=jnp.float32)
    inter_unit, inter_scale = layer_norm(inter)
    inter_norm = (inter_unit * fm_gain).astype(jnp.bfloat16)
    inter_rows = inter_norm.reshape(samples * NF, -1)
    row_total = inter_rows.shape[0]
    up_all, down_all = (
        lax.all_gather(w_up, "wide", axis=0, tiled=True),
        lax.all_gather(w_down, "wide", axis=0, tiled=True),
    )
    gate_pre = jnp.einsum("rk,hk->rh", inter_rows, up_all, preferred_element_type=jnp.float32)
    hidden = jax.nn.silu(gate_pre).astype(jnp.bfloat16)
    ff_rows = jnp.dot(hidden, down_all, preferred_element_type=jnp.float32)
    linear_out = jnp.einsum("lf,bfe->ble", linear_w, embeds, preferred_element_type=jnp.float32)
    summed = jnp.concatenate(
        [ff_rows.reshape(samples, NF, -1), linear_out], axis=1
    ) + embeds.astype(jnp.float32)
    summed_unit, summed_scale = layer_norm(summed)
    layer_out = (summed_unit * out_gain).astype(jnp.bfloat16)
    grad_summed = norm_back(summed_unit, summed_scale, out_gain, cotangent[0].astype(jnp.float32))
    grad_ff = grad_summed[:, :NF].astype(jnp.bfloat16)
    grad_lin = grad_summed[:, NF:].astype(jnp.bfloat16)
    grad_ff_rows = grad_ff.reshape(row_total, -1)
    grad_hidden = jnp.einsum(
        "re,he->rh", grad_ff_rows, down_all, preferred_element_type=jnp.float32
    )
    grad_gate = (grad_hidden * silu_back(gate_pre)).astype(jnp.bfloat16)
    grad_rows = jnp.dot(grad_gate, up_all, preferred_element_type=jnp.float32)
    rank_width = w_up.shape[1]
    up_term = jnp.einsum("rh,rk->hk", grad_gate, inter_rows, preferred_element_type=jnp.float32)
    down_term_part = jnp.einsum(
        "rh,re->he", hidden, grad_ff_rows, preferred_element_type=jnp.float32
    )
    both_terms = lax.psum_scatter(
        jnp.concatenate([up_term, down_term_part], axis=1), "wide", scatter_dimension=0, tiled=True
    )
    up_local = both_terms[:, :rank_width]
    down_local = both_terms[:, rank_width:]
    grad_up, grad_down = lax.psum((up_local, down_local), "emb")
    grad_norm = grad_rows.reshape(samples, NF, -1)
    grad_inter = norm_back(inter_unit, inter_scale, fm_gain, grad_norm).astype(jnp.bfloat16)
    grad_mixing = jnp.einsum(
        "bnk,bek->bne", grad_inter, crossed, preferred_element_type=jnp.float32
    ).astype(jnp.bfloat16)
    grad_crossed = jnp.einsum(
        "bne,bnk->bek", mixing, grad_inter, preferred_element_type=jnp.float32
    ).astype(jnp.bfloat16)
    grad_embeds = grad_summed + jnp.einsum(
        "lf,ble->bfe", linear_w, grad_lin, preferred_element_type=jnp.float32
    )
    grad_embeds = grad_embeds + jnp.einsum(
        "nf,bne->bfe", proj_p, grad_mixing, preferred_element_type=jnp.float32
    )
    grad_embeds = grad_embeds + jnp.einsum(
        "fk,bek->bfe", proj_y, grad_crossed, preferred_element_type=jnp.float32
    )
    grad_embeds = grad_embeds.astype(jnp.bfloat16)
    slot_grads = grad_embeds[:, slot_field]
    returned = lax.all_to_all(slot_grads[None], "emb", split_axis=2, concat_axis=1, tiled=True)
    return (layer_out[None], returned, grad_up, grad_down)


def solution(mesh):
    placed = (
        P("emb", None, None),
        P("wide", None, "emb", None),
        P("wide", None, "emb"),
        P(),
        P(),
        P(),
        P(),
        P(),
        P("wide", None),
        P("wide", None),
        P(),
        P("wide", "emb", None, None),
    )
    return jax.shard_map(
        body,
        mesh=mesh,
        in_specs=placed,
        out_specs=(
            P("wide", "emb", None, None),
            P("wide", None, "emb", None),
            P("wide", None),
            P("wide", None),
        ),
        check_vma=False,
    )
```

profile of v0, /device:TPU:3, one launch (start us, length us, event | category | flops | bytes accessed | tf_op | source)
XLA Modules:
  0.0 922.4 jit_solution(3896068090639616225)
XLA Ops:
  7.2 0.7 all-gather.3.cloned.1.call-update
  8.0 0.7 all-gather.5.cloned.1.call-update
  8.7 0.8 compare_select_fusion
  9.5 0.9 compare_and_fusion
  10.4 0.5 copy.67
  10.9 0.6 reshape.112
  11.6 33.8 %gather_fusion = bf16[8192,256]{1,0:T(8,128)(2,1)} fusion(bf16[8192,256]{1,0:T(8,128)(2,1)} %bitcast.109, s32[8192]{0:T(1024)S(1)} %broadcast_clamp_fusion), kind=kCustom, calls=%fused_computation | custom fusion | bytes 8421376 | tf_op jit(solution)/shard_map/jit(_take)/gather | solution.py:37
  45.4 7.0 reshape.111
  52.4 0.6 copy.66
  53.0 0.1 copy.65
  53.1 0.3 fusion.15
  53.4 8.1 fusion
  61.5 1.2 copy.95
  62.8 11.9 %all-to-all-start = ((bf16[1,128,16,256]{3,2,0,1:T(8,128)(2,1)}), bf16[1,128,16,256]{3,2,0,1:T(8,128)(2,1)S(1)}, u32[]{:S(2)}, u32[]{:S(2)}) async-start(bf16[1,128,16,256]{3,2,0,1:T(8,128)(2,1)} %bitcast.108), calls=%async_computation | async-start | bytes 2097152 | tf_op jit(solution)/shard_map/all_to_all | solution.py:61
  74.8 1.3 copy.76
  76.1 38.5 %all-to-all-done = bf16[1,128,16,256]{3,2,0,1:T(8,128)(2,1)S(1)} async-done(((bf16[1,128,16,256]{3,2,0,1:T(8,128)(2,1)}), bf16[1,128,16,256]{3,2,0,1:T(8,128)(2,1)S(1)}, u32[]{:S(2)}, u32[]{:S(2)}) %all-to-all-start) | async-done | bytes 1048608 | tf_op jit(solution)/shard_map/all_to_all | solution.py:61
  114.6 0.1 copy.68
  114.7 0.8 copy.69
  115.5 0.3 broadcast_in_dim.20
  115.8 13.6 %scatter_fusion = bf16[4,512,256]{2,0,1:T(4,128)(2,1)S(1)} fusion(bf16[4,512,256]{2,0,1:T(4,128)(2,1)S(1)} %broadcast_in_dim.20, s32[512]{0:T(512)S(1)} %compare_select_fusion.2, bf16[512,4,256]{2,1,0:T(4,128)(2,1)S(1)} %copy.69), kind=kCustom, calls=%fused_computation.2 | custom fusion | bytes 3147776 | tf_op jit(solution)/shard_map/scatter | solution.py:63
  129.4 1.0 copy.70
  130.4 1.3 convolution_convert_fusion.3
  131.7 1.5 convolution_convert_fusion
  133.2 0.4 fusion.28
  133.6 0.2 multiply_reduce_fusion.3
  133.9 0.5 copy-done.3
  134.4 0.5 copy-done.19
  134.9 0.2 multiply_convert_fusion.4
  135.2 1.9 convolution_bitcast_fusion
  137.1 13.2 %multiply_convert_fusion.1 = (bf16[512,8192]{1,0:T(8,128)(2,1)}, f32[512,8192]{1,0:T(8,128)}) fusion(bf16[512,256]{1,0:T(8,128)(2,1)S(1)} %bitcast.114, bf16[8192,256]{1,0:T(8,128)(2,1)} %all-gather.3.cloned.1.call-done), kind=kOutput, calls=%fused_computation.5 | convolution fusion | flops 2168455168 | bytes 29622272 | tf_op jit(solution)/shard_map/rk,hk->rh/dot_general | solution.py:80
  150.2 72.4 %all-gather.5.cloned.1.call-done = bf16[8192,256]{1,0:T(8,128)(2,1)} async-done(((bf16[1024,256]{1,0:T(8,128)(2,1)}), bf16[8192,256]{1,0:T(8,128)(2,1)}) %all-gather.5.cloned.1.call-update) | async-done | bytes 4194320 | tf_op jit(solution)/shard_map/all_gather | solution.py:78
  222.7 6.9 fusion.29
  229.6 1.0 copy.74
  230.6 1.9 fusion.26
  232.5 0.3 multiply_reduce_fusion
  232.9 0.6 fusion.6
  233.5 1.9 fusion.22
  235.4 1.0 copy-done.8
  236.4 0.1 copy.77
  236.6 5.8 fusion.31
  242.4 13.6 %multiply_convert_fusion = bf16[512,8192]{1,0:T(8,128)(2,1)} fusion(f32[512,8192]{1,0:T(8,128)} %get-tuple-element.33, bf16[512,256]{1,0:T(8,128)(2,1)S(1)} %bitcast.117, bf16[8192,256]{1,0:T(8,128)(2,1)} %all-gather.5.cloned.1.call-done), kind=kOutput, calls=%fused_computation.4 | convolution fusion | flops 2185232384 | bytes 29622272 | tf_op jit(solution)/shard_map/re,he->rh/dot_general | solution.py:93
  256.0 6.0 fusion.30
  262.0 6.2 pad_maximum_fusion
  268.2 0.6 copy-done.22
  268.8 0.6 pad_clamp_fusion
  269.4 7.1 multiply_reduce_fusion.2
  276.6 0.3 multiply_reduce_fusion.1
  276.9 0.3 multiply_convert_fusion.3
  277.2 0.7 copy-done.10
  277.9 2.0 fusion.12
  280.0 3.4 fusion.16
  283.4 315.0 %reduce-scatter.2.cloned.1.call-done = f32[1024,512]{0,1:T(8,128)} async-done(((f32[8192,512]{0,1:T(8,128)}), f32[1024,512]{0,1:T(8,128)}) %reduce-scatter.2.cloned.1.call-update) | async-done | bytes 2097168 | tf_op jit(solution)/shard_map/reduce_scatter | solution.py:103
  598.4 3.1 fusion.27
  601.5 4.5 fusion.10
  606.0 1.8 copy.79
  607.8 3.1 gather_fusion.1
  610.8 9.3 %all-to-all-start.1 = ((bf16[1,4,512,256]{3,1,0,2:T(4,128)(2,1)}), bf16[1,4,512,256]{3,1,0,2:T(4,128)(2,1)S(1)}, u32[]{:S(2)}, u32[]{:S(2)}) async-start(bf16[1,4,512,256]{3,1,0,2:T(4,128)(2,1)} %bitcast.27), calls=%async_computation.1 | async-start | bytes 2097152 | tf_op jit(solution)/shard_map/all_to_all | solution.py:128
  620.2 1.3 copy.83
  621.5 22.7 %all-to-all-done.1 = bf16[1,4,512,256]{3,1,0,2:T(4,128)(2,1)S(1)} async-done(((bf16[1,4,512,256]{3,1,0,2:T(4,128)(2,1)}), bf16[1,4,512,256]{3,1,0,2:T(4,128)(2,1)S(1)}, u32[]{:S(2)}, u32[]{:S(2)}) %all-to-all-start.1) | async-done | bytes 1048608 | tf_op jit(solution)/shard_map/all_to_all | solution.py:128
  644.2 0.1 copy.81
  644.3 1.1 copy.82
  645.4 265.4 %all-reduce.3.cloned.1.call-done = (f32[1024,256]{0,1:T(8,128)}, f32[1024,256]{0,1:T(8,128)}) async-done(((f32[1024,256]{0,1:T(8,128)}, f32[1024,256]{0,1:T(8,128)}), (f32[1024,256]{0,1:T(8,128)}, f32[1024,256]{0,1:T(8,128)})) %all-reduce.3.cloned.1.call-update) | async-done | bytes 2097168 | tf_op jit(solution)/shard_map/psum | solution.py:108
  910.8 2.5 copy.84
  913.3 2.5 copy.85
  (69 shorter events, 0.4 us)
Async XLA Ops:
  7.2 128.0 %copy-start = (bf16[384,512]{1,0:T(8,128)(2,1)S(1)}, bf16[384,512]{1,0:T(8,128)(2,1)}, u32[]{:S(2)}) copy-start(bf16[384,512]{1,0:T(8,128)(2,1)} %param.18) | copy-start | bytes 1179652
  7.2 129.9 %all-gather.3.cloned.1.call-start = ((), (), s32[]{:S(2)}) async-start(), calls=%async_computation.3 | async-start | bytes 4718592 | tf_op jit(solution)/shard_map/all_gather | solution.py:77
  7.9 214.8 %all-gather.5.cloned.1.call-start = ((), (), s32[]{:S(2)}) async-start(), calls=%async_computation.4 | async-start | bytes 4718592 | tf_op jit(solution)/shard_map/all_gather | solution.py:78
  45.4 7.6 copy-start.26
  61.5 13.3 %copy-start.13 = (bf16[1,4,512,256]{3,2,1,0:T(8,128)(2,1)S(1)}, bf16[1,4,512,256]{3,2,1,0:T(8,128)(2,1)}, u32[]{:S(2)}) copy-start(bf16[1,4,512,256]{3,2,1,0:T(8,128)(2,1)} %param.23) | copy-start | bytes 3145732
  61.5 14.6 %copy-start.27 = (s32[512]{0:T(512)S(1)}, s32[512]{0:T(512)}, u32[]{:S(2)}) copy-start(s32[512]{0:T(512)} %param.15) | copy-start | bytes 6148
  62.8 51.9 %all-to-all-start = ((bf16[1,128,16,256]{3,2,0,1:T(8,128)(2,1)}), bf16[1,128,16,256]{3,2,0,1:T(8,128)(2,1)S(1)}, u32[]{:S(2)}, u32[]{:S(2)}) async-start(bf16[1,128,16,256]{3,2,0,1:T(8,128)(2,1)} %bitcast.108), calls=%async_computation | async-start | bytes 2097152 | tf_op jit(solution)/shard_map/all_to_all | solution.py:61
  74.7 523.7 %reduce-scatter.2.cloned.1.call-start = ((), (), s32[]{:S(2)}) async-start(), calls=%async_computation.5 | async-start | bytes 18874368 | tf_op jit(solution)/shard_map/reduce_scatter | solution.py:103
  76.1 39.7 %copy-start.21 = (s32[512]{0:T(512)}, s32[512]{0:T(512)S(1)}, u32[]{:S(2)}) copy-start(s32[512]{0:T(512)S(1)} %compare_select_fusion.2) | copy-start | bytes 6148
  129.4 5.5 copy-start.23
  131.7 3.4 copy-start.9
  133.2 1.9 copy-start.5
  133.6 0.8 copy-start.3
  133.6 0.8 copy-start.17
  134.4 0.5 copy-start.19
  135.2 15.1 %copy-start.11 = (bf16[4,128,256]{2,1,0:T(8,128)(2,1)}, bf16[4,128,256]{2,1,0:T(8,128)(2,1)S(1)}, u32[]{:S(2)}) copy-start(bf16[4,128,256]{2,1,0:T(8,128)(2,1)S(1)} %multiply_convert_fusion.4) | copy-start | bytes 786436
  230.6 2.3 copy-start.1
  230.6 2.3 copy-start.25
  233.5 1.9 copy-start.15
  233.5 1.9 copy-start.16
  235.4 1.0 copy-start.8
  242.4 13.6 %copy-start.12 = (bf16[4,128,256]{2,1,0:T(8,128)(2,1)S(1)}, bf16[4,128,256]{2,1,0:T(8,128)(2,1)}, u32[]{:S(2)}) copy-start(bf16[4,128,256]{2,1,0:T(8,128)(2,1)} %copy-done.11) | copy-start | bytes 786436
  268.1 0.7 copy-start.22
  268.1 1.3 copy-start.24
  268.2 642.6 %all-reduce.3.cloned.1.call-start = ((), (), s32[]{:S(2)}) async-start(), calls=%async_computation.6 | async-start | bytes 4194304 | tf_op jit(solution)/shard_map/psum | solution.py:108
  269.4 7.1 copy-start.4
  269.4 7.1 copy-start.18
  269.4 7.1 copy-start.20
  269.4 8.5 copy-start.6
  269.4 8.5 copy-start.14
  277.2 0.7 copy-start.10
  280.0 321.6 %copy-start.2 = (bf16[1,4,512,256]{2,3,1,0:T(8,128)(2,1)S(1)}, bf16[1,4,512,256]{2,3,1,0:T(8,128)(2,1)}, u32[]{:S(2)}) copy-start(bf16[1,4,512,256]{2,3,1,0:T(8,128)(2,1)} %copy.76) | copy-start | bytes 3145732
  606.0 14.2 %copy-start.7 = (bf16[1,4,512,256]{2,3,1,0:T(8,128)(2,1)S(1)}, bf16[1,4,512,256]{2,3,1,0:T(8,128)(2,1)}, u32[]{:S(2)}) copy-start(bf16[1,4,512,256]{2,3,1,0:T(8,128)(2,1)} %get-tuple-element.27) | copy-start | bytes 3145732
  610.8 33.3 %all-to-all-start.1 = ((bf16[1,4,512,256]{3,1,0,2:T(4,128)(2,1)}), bf16[1,4,512,256]{3,1,0,2:T(4,128)(2,1)S(1)}, u32[]{:S(2)}, u32[]{:S(2)}) async-start(bf16[1,4,512,256]{3,1,0,2:T(4,128)(2,1)} %bitcast.27), calls=%async_computation.1 | async-start | bytes 2097152 | tf_op jit(solution)/shard_map/all_to_all | solution.py:128
Sparse Core Ops, SparseCore 0:
  9.8 117.7 all-gather.2
  129.4 93.2 all-gather.4
  268.3 330.0 reduce-scatter.1
  601.6 309.1 all-reduce.2
where the time goes:
time: 924 us; the launch traced here: 922 us
  waiting for transfers between devices  715 us (77%)
  local copies, waits for them, and re-layouts  81.1 us (9%)
  matrix products  75.6 us (8%)
  starting transfers between devices  21.4 us (2%)
  other arithmetic  14.7 us (2%)
  between operations  14.2 us (2%)
    reduce_scatter x1, waiting for transfers between devices, body(): lax.psum_scatter(jnp.concatenate([up_term, down_term_part], axis=1), 'wid...  315 us
    psum x1, waiting for transfers between devices, body(): grad_up, grad_down = lax.psum((up_local, down_local), 'emb')  265 us
    all_gather x1, waiting for transfers between devices, body(): lax.all_gather(w_down, 'wide', axis=0, tiled=True)  72.4 us
    gather x2, local copies, waits for them, and re-layouts, pool_bags(): jnp.take(tables.reshape(slots_here * bucket_count, -1), flat_ids, axis=0)  40.8 us
    all_to_all x1, waiting for transfers between devices, body(): lax.all_to_all(pooled, 'emb', split_axis=1, concat_axis=2, tiled=True)  38.5 us
    all_to_all x1, waiting for transfers between devices, body(): lax.all_to_all(slot_grads[None], 'emb', split_axis=2, concat_axis=1, tile...  22.7 us
  transfers between devices with their start and end apart: 6, of which 5 were waited for; matrix products, arithmetic and copies ran while one was open for 13% of the time, Pallas kernels for 0%

commit v1 on v0

v1 whole, which is shorter than its diff:
```python
import functools

import jax
import jax.numpy as jnp
from jax import lax
from jax.experimental import pallas as pl
from jax.experimental.pallas import tpu as pltpu
from jax.sharding import PartitionSpec as P

MESH = pl.DeviceIdType.MESH
F32 = jnp.float32
BF16 = jnp.bfloat16

E = 256
FIELDS = 512
ROWS = 512
NF = 128
NL = 384
BAG = 4
SAMPLES = 4
SLOTS = 16
GROUP_B = 128
EMB = 32
XS = 4
YS = 4
ZS = 4
SLICE = 1024
TH = 512
TILES = 8
NROW = SAMPLES * NF
norm_eps = 1e-05


def dot(a, b, ca=1, cb=0):
    return lax.dot_general(a, b, (((ca,), (cb,)), ((), ())), preferred_element_type=F32)


def send(src, dst, send_sem, recv_sem, **device):
    return pltpu.make_async_remote_copy(
        src_ref=src,
        dst_ref=dst,
        send_sem=send_sem,
        recv_sem=recv_sem,
        device_id=device,
        device_id_type=MESH,
    )


def signal(sem, **device):
    pl.semaphore_signal(sem, inc=1, device_id=device, device_id_type=MESH)


def norm_forward(values):
    centre = jnp.mean(values, axis=-1, keepdims=True)
    shifted = values - centre
    scale = lax.rsqrt(jnp.mean(shifted * shifted, axis=-1, keepdims=True) + norm_eps)
    return shifted * scale, scale


def norm_back(unit, scale, gain, upstream):
    scaled = upstream * gain
    return scale * (
        scaled
        - jnp.mean(scaled, axis=-1, keepdims=True)
        - unit * jnp.mean(scaled * unit, axis=-1, keepdims=True)
    )


def pool_kernel(
    ids, lengths, tables, w_up, w_down, slots_out, up_all, down_all,
    held, pooled, outgoing, table_sem, bag_send, bag_recv, w_send, w_recv, w_local,
):
    me = lax.axis_index("emb")
    wide = lax.axis_index("wide")
    x = wide // 2
    z_lo = lax.rem(wide, 2)

    def fetch(s):
        return pltpu.make_async_copy(tables.at[s], held.at[s], table_sem.at[s])

    @pl.loop(0, SLOTS)
    def _(s):
        fetch(s).start()

    barrier = pltpu.get_barrier_semaphore()

    @pl.loop(1, EMB)
    def _(k):
        signal(barrier, emb=lax.rem(me + k, EMB))

    for k in range(1, XS):
        signal(barrier, wide=lax.rem(x + k, XS) * 2 + z_lo)
    pl.semaphore_wait(barrier, EMB - 1 + XS - 1)

    weights = ((w_up, up_all), (w_down, down_all))
    local = [
        pltpu.make_async_copy(w, full.at[x], w_local.at[i]) for i, (w, full) in enumerate(weights)
    ]
    remote = [
        send(w, full.at[x], w_send.at[i, k - 1], w_recv.at[i, k - 1], wide=lax.rem(x + k, XS) * 2 + z_lo)
        for k in range(1, XS)
        for i, (w, full) in enumerate(weights)
    ]
    for copy in remote + local:
        copy.start()

    bucket = lax.broadcasted_iota(jnp.int32, (ROWS, GROUP_B), 0)

    for s in range(SLOTS):
        fetch(s).wait()
        live = lengths[s : s + 1, :]
        counts = jnp.zeros((ROWS, GROUP_B), F32)
        for j in range(BAG):
            wanted = jnp.where(live > j, ids[s, j : j + 1, :], -1)
            counts = counts + jnp.where(bucket == wanted, 1.0, 0.0)
        rows = dot(counts.astype(BF16), held[s], 0, 0)
        for half in range(2):
            pooled[half, pl.ds(s, GROUP_B, stride=SLOTS), :] = rows[:, half * 128 : half * 128 + 128]

    for half in range(2):
        outgoing[:, :, half * 128 : half * 128 + 128] = (
            pooled[half].astype(BF16).reshape(GROUP_B, SLOTS, 128)
        )

    mine = pl.ds(pl.multiple_of(me * SLOTS, SLOTS), SLOTS)

    def bags(k):
        peer = lax.rem(me + k, EMB)
        return send(
            outgoing.at[pl.ds(peer * SAMPLES, SAMPLES)],
            slots_out.at[:, mine, :],
            bag_send.at[k],
            bag_recv.at[k],
            emb=peer,
        )

    @pl.loop(1, EMB)
    def _(k):
        bags(k).start()

    slots_out[:, mine, :] = outgoing[pl.ds(me * SAMPLES, SAMPLES)]

    @pl.loop(1, EMB)
    def _(k):
        source = lax.rem(me + EMB - k, EMB)
        there = pl.ds(pl.multiple_of(source * SLOTS, SLOTS), SLOTS)
        send(
            outgoing.at[pl.ds(source * SAMPLES, SAMPLES)],
            slots_out.at[:, there, :],
            bag_send.at[k],
            bag_recv.at[k],
            emb=source,
        ).wait_recv()
        bags(k).wait_send()

    for copy in local:
        copy.wait()
    for copy in remote:
        copy.wait_send()
    for k in range(1, XS):
        source = lax.rem(x + XS - k, XS)
        for i, (w, full) in enumerate(weights):
            send(
                w, full.at[source], w_send.at[i, k - 1], w_recv.at[i, k - 1], wide=source * 2 + z_lo
            ).wait_recv()


def pool_and_gather(ids, lengths, tables, w_up, w_down):
    any_space = pl.BlockSpec(memory_space=pl.ANY)
    vmem = pl.BlockSpec(memory_space=pltpu.VMEM)
    return pl.pallas_call(
        pool_kernel,
        name="pool_and_gather",
        out_shape=(
            jax.ShapeDtypeStruct((SAMPLES, FIELDS, E), BF16),
            jax.ShapeDtypeStruct((XS, SLICE, E), BF16),
            jax.ShapeDtypeStruct((XS, SLICE, E), BF16),
        ),
        in_specs=[vmem, vmem, any_space, any_space, any_space],
        out_specs=(vmem, any_space, any_space),
        scratch_shapes=[
            pltpu.VMEM((SLOTS, ROWS, E), BF16),
            pltpu.VMEM((2, GROUP_B * SLOTS, 128), F32),
            pltpu.VMEM((GROUP_B, SLOTS, E), BF16),
            pltpu.SemaphoreType.DMA((SLOTS,)),
            pltpu.SemaphoreType.DMA((EMB,)),
            pltpu.SemaphoreType.DMA((EMB,)),
            pltpu.SemaphoreType.DMA((2, XS - 1)),
            pltpu.SemaphoreType.DMA((2, XS - 1)),
            pltpu.SemaphoreType.DMA((2,)),
        ],
        compiler_params=pltpu.CompilerParams(
            collective_id=0, has_side_effects=True, vmem_limit_bytes=32 << 20
        ),
    )(ids, lengths, tables, w_up, w_down)


def layer_kernel(
    slots, field_row, field_column, proj_y, proj_p, linear_w, fm_gain, w_up, w_down, out_gain, cotangent,
    layer_out, slot_grads, grads,
    embeds, crossed, mixing, inter_unit, inter_scale, rows, rows_t, hidden, slope, ff, ff_out, ff_in,
    linear_out, grad_summed, grad_rows, grad_rows_t, grad_lin, weight_sum, norm_out, norm_in,
    send_sem, recv_sem,
):
    wide = lax.axis_index("wide")
    partner = wide + 1 - 2 * lax.rem(wide, 2)

    barrier = pltpu.get_barrier_semaphore()
    signal(barrier, wide=partner)

    def exchange(src, dst, n):
        return send(src, dst, send_sem.at[n], recv_sem.at[n], wide=partner)

    by_field = jnp.where(
        lax.broadcasted_iota(jnp.int32, (FIELDS, FIELDS), 0) == field_row[...], 1.0, 0.0
    ).astype(BF16)

    def embed(b, _):
        x = dot(by_field, slots[b]).astype(BF16)
        embeds[b] = x
        cross = dot(x, proj_y[...], 0, 0).astype(BF16)
        crossed[b] = cross
        mix = dot(proj_p[...], x).astype(BF16)
        mixing[b] = mix
        unit, scale = norm_forward(dot(mix, cross))
        inter_unit[b] = unit
        inter_scale[b] = jnp.broadcast_to(scale, (NF, 128))
        rows[0, pl.ds(pl.multiple_of(b * NF, NF), NF), :] = (unit * fm_gain[...]).astype(BF16)
        return 0

    lax.fori_loop(0, SAMPLES, embed, 0)

    pl.semaphore_wait(barrier, 1)
    rows_copy = exchange(rows.at[0], rows.at[1], 0)
    rows_copy.start()

    ff[...] = jnp.zeros_like(ff)

    def forward(group, tile):
        gate = dot(rows[group], w_up[tile], 1, 1)
        sigma = 0.5 * jnp.tanh(0.5 * gate) + 0.5
        act = gate * sigma
        slope[group, tile] = (sigma + act * (1.0 - sigma)).astype(BF16)
        act = act.astype(BF16)
        hidden[group, tile] = act
        ff[group] += dot(act, w_down[tile])

    def forward_tiles(group, first, last):
        @pl.loop(first, last)
        def _(tile):
            forward(group, tile)

    forward_tiles(0, 0, TILES // 2)

    def linear(b, _):
        linear_out[b] = dot(linear_w[...], embeds[b])
        return 0

    lax.fori_loop(0, SAMPLES, linear, 0)
    rows_copy.wait()
    forward_tiles(1, 0, TILES)
    ff_out[...] = ff[1].astype(BF16)
    ff_copy = exchange(ff_out, ff_in, 1)
    ff_copy.start()
    forward_tiles(0, TILES // 2, TILES)
    rows_t[0] = rows[0].astype(F32).T.astype(BF16)
    rows_t[1] = rows[1].astype(F32).T.astype(BF16)
    ff_copy.wait()

    def finish(values, b, first, count):
        here = slice(first, first + count)
        unit, scale = norm_forward(values + embeds[b, here, :].astype(F32))
        layer_out[b, here, :] = (unit * out_gain[...]).astype(BF16)
        grad = norm_back(unit, scale, out_gain[...], cotangent[b, here, :].astype(F32))
        grad_summed[b, here, :] = grad
        return grad.astype(BF16)

    def finish_ff(b, _):
        mine = pl.ds(pl.multiple_of(b * NF, NF), NF)
        total = ff[0, mine, :] + ff_in[mine, :].astype(F32)
        grad_rows[0, mine, :] = finish(total, b, 0, NF)
        return 0

    lax.fori_loop(0, SAMPLES, finish_ff, 0)
    grad_copy = exchange(grad_rows.at[0], grad_rows.at[1], 2)
    grad_copy.start()

    def finish_linear(b, _):
        grad_lin[b] = finish(linear_out[b], b, NF, NL)
        grad_summed[b] += dot(linear_w[...], grad_lin[b], 0, 0)
        return 0

    lax.fori_loop(0, SAMPLES, finish_linear, 0)
    grad_rows_t[0] = grad_rows[0].astype(F32).T.astype(BF16)
    grad_copy.wait()
    grad_rows_t[1] = grad_rows[1].astype(F32).T.astype(BF16)

    ff[...] = jnp.zeros_like(ff)

    def backward(group, tile):
        grad_gate = (dot(grad_rows[group], w_down[tile], 1, 1) * slope[group, tile].astype(F32)).astype(BF16)
        ff[group] += dot(grad_gate, w_up[tile])
        up = dot(rows_t[group], grad_gate)
        down = dot(grad_rows_t[group], hidden[group, tile])
        return up, down

    @pl.loop(0, TILES)
    def _(tile):
        up, down = backward(1, tile)
        weight_sum[0, tile] = up
        weight_sum[1, tile] = down

    norm_out[...] = ff[1].astype(BF16)
    norm_copy = exchange(norm_out, norm_in, 3)
    norm_copy.start()

    @pl.loop(0, TILES)
    def _(tile):
        up, down = backward(0, tile)
        for kind, part in enumerate((up, down)):
            whole = (weight_sum[kind, tile] + part).astype(BF16)
            for half in range(2):
                grads[kind, tile * 2 + half] = whole[:, half * 256 : (half + 1) * 256]

    norm_copy.wait()

    by_slot = jnp.where(
        lax.broadcasted_iota(jnp.int32, (FIELDS, FIELDS), 1) == field_column[...], 1.0, 0.0
    ).astype(BF16)

    def tail(b, _):
        mine = pl.ds(pl.multiple_of(b * NF, NF), NF)
        upstream = ff[0, mine, :] + norm_in[mine, :].astype(F32)
        grad_inter = norm_back(inter_unit[b], inter_scale[b, :, 0:1], fm_gain[...], upstream).astype(BF16)
        grad_mixing = dot(grad_inter, crossed[b], 1, 1).astype(BF16)
        grad_crossed = dot(mixing[b], grad_inter, 0, 0).astype(BF16)
        total = grad_summed[b] + dot(proj_p[...], grad_mixing, 0, 0)
        total = total + dot(proj_y[...], grad_crossed, 1, 1)
        slot_grads[b] = dot(by_slot, total.astype(BF16)).astype(BF16)
        return 0

    lax.fori_loop(0, SAMPLES, tail, 0)


def layer(*operands):
    vmem = pl.BlockSpec(memory_space=pltpu.VMEM)
    return pl.pallas_call(
        layer_kernel,
        name="layer",
        out_shape=(
            jax.ShapeDtypeStruct((SAMPLES, FIELDS, E), BF16),
            jax.ShapeDtypeStruct((SAMPLES, FIELDS, E), BF16),
            jax.ShapeDtypeStruct((2, TILES * 2, 256, 256), BF16),
        ),
        in_specs=[vmem] * len(operands),
        out_specs=(vmem,) * 3,
        scratch_shapes=[
            pltpu.VMEM((SAMPLES, FIELDS, E), BF16),
            pltpu.VMEM((SAMPLES, E, E), BF16),
            pltpu.VMEM((SAMPLES, NF, E), BF16),
            pltpu.VMEM((SAMPLES, NF, E), F32),
            pltpu.VMEM((SAMPLES, NF, 128), F32),
            pltpu.VMEM((2, NROW, E), BF16),
            pltpu.VMEM((2, E, NROW), BF16),
            pltpu.VMEM((2, TILES, NROW, TH), BF16),
            pltpu.VMEM((2, TILES, NROW, TH), BF16),
            pltpu.VMEM((2, NROW, E), F32),
            pltpu.VMEM((NROW, E), BF16),
            pltpu.VMEM((NROW, E), BF16),
            pltpu.VMEM((SAMPLES, NL, E), F32),
            pltpu.VMEM((SAMPLES, FIELDS, E), F32),
            pltpu.VMEM((2, NROW, E), BF16),
            pltpu.VMEM((2, E, NROW), BF16),
            pltpu.VMEM((SAMPLES, NL, E), BF16),
            pltpu.VMEM((2, TILES, E, TH), F32),
            pltpu.VMEM((NROW, E), BF16),
            pltpu.VMEM((NROW, E), BF16),
            pltpu.SemaphoreType.DMA((4,)),
            pltpu.SemaphoreType.DMA((4,)),
        ],
        compiler_params=pltpu.CompilerParams(
            collective_id=1, has_side_effects=True, vmem_limit_bytes=60 << 20
        ),
    )(*operands)


def reduce_kernel(
    slot_grads, grads, bag_grads, up_out, down_out,
    from_core, to_x, from_x, to_y, from_y, to_z, from_z, whole,
    bag_send, bag_recv, send_sem, recv_sem,
):
    me = lax.axis_index("emb")
    wide = lax.axis_index("wide")
    x = wide // 2
    z_lo = lax.rem(wide, 2)
    core = lax.rem(me, 2)
    y = lax.rem(me // 2, YS)
    z = me // (2 * YS)
    sibling = me + 1 - 2 * core

    def emb_at(z_at, y_at):
        return (z_at * YS + y_at) * 2 + core

    barrier = pltpu.get_barrier_semaphore()

    @pl.loop(1, EMB)
    def _(k):
        signal(barrier, emb=lax.rem(me + k, EMB))

    for k in range(1, XS):
        signal(barrier, wide=lax.rem(x + k, XS) * 2 + z_lo)
    pl.semaphore_wait(barrier, EMB - 1 + XS - 1)

    core_copy = send(grads.at[1 - core], from_core, send_sem.at[0], recv_sem.at[0], emb=sibling)
    core_copy.start()

    def bags(k):
        peer = lax.rem(me + k, EMB)
        return send(
            slot_grads.at[:, pl.ds(pl.multiple_of(peer * SLOTS, SLOTS), SLOTS), :],
            bag_grads.at[pl.ds(me * SAMPLES, SAMPLES)],
            bag_send.at[k],
            bag_recv.at[k],
            emb=peer,
        )

    @pl.loop(1, EMB)
    def _(k):
        bags(k).start()

    bag_grads[pl.ds(me * SAMPLES, SAMPLES)] = slot_grads[:, pl.ds(pl.multiple_of(me * SLOTS, SLOTS), SLOTS), :]

    core_copy.wait()

    @pl.loop(0, TILES * 2)
    def _(t):
        to_x[t] = (grads[core, t].astype(F32) + from_core[t].astype(F32)).astype(BF16)

    x_copies = []
    for k in range(1, XS):
        peer = lax.rem(x + k, XS)
        x_copies.append(
            send(
                to_x.at[pl.ds(peer * 4, 4)],
                from_x.at[k - 1],
                send_sem.at[k],
                recv_sem.at[k],
                wide=peer * 2 + z_lo,
            )
        )
    for copy in x_copies:
        copy.start()
    for copy in x_copies:
        copy.wait()

    @pl.loop(0, 4)
    def _(t):
        mine = x * 4 + t
        total = grads[core, mine].astype(F32) + from_core[mine].astype(F32)
        for k in range(XS - 1):
            total = total + from_x[k, t].astype(F32)
        to_y[t] = total.astype(BF16)

    y_copies = []
    for k in range(1, YS):
        peer = lax.rem(y + k, YS)
        y_copies.append(
            send(to_y.at[peer], from_y.at[k - 1], send_sem.at[3 + k], recv_sem.at[3 + k], emb=emb_at(z, peer))
        )
    for copy in y_copies:
        copy.start()
    for copy in y_copies:
        copy.wait()

    total = to_y[y].astype(F32)
    for k in range(YS - 1):
        total = total + from_y[k].astype(F32)
    for part in range(ZS):
        to_z[part] = total[
            (part % 2) * 128 : (part % 2) * 128 + 128, (part // 2) * 128 : (part // 2) * 128 + 128
        ].astype(BF16)

    z_copies = []
    for k in range(1, ZS):
        peer = lax.rem(z + k, ZS)
        z_copies.append(
            send(to_z.at[peer], from_z.at[k - 1], send_sem.at[6 + k], recv_sem.at[6 + k], emb=emb_at(peer, y))
        )
    for copy in z_copies:
        copy.start()
    for copy in z_copies:
        copy.wait()

    total = to_z[z].astype(F32)
    for k in range(ZS - 1):
        total = total + from_z[k].astype(F32)

    def piece(z_at):
        row = pl.multiple_of(y * 256 + (z_at // 2) * 128, 128)
        column = pl.multiple_of(lax.rem(z_at, 2) * 128, 128)
        return whole.at[core, pl.ds(row, 128), pl.ds(column, 128)]

    row = pl.multiple_of(y * 256 + (z // 2) * 128, 128)
    column = pl.multiple_of(lax.rem(z, 2) * 128, 128)
    whole[core, pl.ds(row, 128), pl.ds(column, 128)] = total.T.astype(BF16)

    for k in range(1, ZS):
        send(
            piece(z), piece(z), send_sem.at[9 + k], recv_sem.at[9 + k], emb=emb_at(lax.rem(z + k, ZS), y)
        ).start()
    for k in range(1, ZS):
        source = lax.rem(z + ZS - k, ZS)
        copy = send(piece(z), piece(source), send_sem.at[9 + k], recv_sem.at[9 + k], emb=emb_at(source, y))
        copy.wait_send()
        copy.wait_recv()

    def band(y_at):
        return whole.at[core, pl.ds(pl.multiple_of(y_at * 256, 256), 256), :]

    for k in range(1, YS):
        send(
            band(y), band(y), send_sem.at[12 + k], recv_sem.at[12 + k], emb=emb_at(z, lax.rem(y + k, YS))
        ).start()
    for k in range(1, YS):
        source = lax.rem(y + YS - k, YS)
        copy = send(band(y), band(source), send_sem.at[12 + k], recv_sem.at[12 + k], emb=emb_at(z, source))
        copy.wait_send()
        copy.wait_recv()

    send(whole.at[core], whole.at[core], send_sem.at[16], recv_sem.at[16], emb=sibling).start()
    copy = send(whole.at[core], whole.at[1 - core], send_sem.at[16], recv_sem.at[16], emb=sibling)
    copy.wait_send()
    copy.wait_recv()
    up_out[...] = whole[0].astype(F32)
    down_out[...] = whole[1].astype(F32)

    @pl.loop(1, EMB)
    def _(k):
        source = lax.rem(me + EMB - k, EMB)
        send(
            slot_grads.at[:, pl.ds(pl.multiple_of(source * SLOTS, SLOTS), SLOTS), :],
            bag_grads.at[pl.ds(source * SAMPLES, SAMPLES)],
            bag_send.at[k],
            bag_recv.at[k],
            emb=source,
        ).wait_recv()
        bags(k).wait_send()


def reduce_and_return(slot_grads, grads):
    vmem = pl.BlockSpec(memory_space=pltpu.VMEM)
    return pl.pallas_call(
        reduce_kernel,
        name="reduce_and_return",
        out_shape=(
            jax.ShapeDtypeStruct((GROUP_B, SLOTS, E), BF16),
            jax.ShapeDtypeStruct((SLICE, E), F32),
            jax.ShapeDtypeStruct((SLICE, E), F32),
        ),
        in_specs=[vmem, vmem],
        out_specs=(vmem,) * 3,
        scratch_shapes=[
            pltpu.VMEM((TILES * 2, 256, 256), BF16),
            pltpu.VMEM((TILES * 2, 256, 256), BF16),
            pltpu.VMEM((XS - 1, 4, 256, 256), BF16),
            pltpu.VMEM((YS, 256, 256), BF16),
            pltpu.VMEM((YS - 1, 256, 256), BF16),
            pltpu.VMEM((ZS, 128, 128), BF16),
            pltpu.VMEM((ZS - 1, 128, 128), BF16),
            pltpu.VMEM((2, SLICE, E), BF16),
            pltpu.SemaphoreType.DMA((EMB,)),
            pltpu.SemaphoreType.DMA((EMB,)),
            pltpu.SemaphoreType.DMA((17,)),
            pltpu.SemaphoreType.DMA((17,)),
        ],
        compiler_params=pltpu.CompilerParams(
            collective_id=2, has_side_effects=True, vmem_limit_bytes=48 << 20
        ),
    )(slot_grads, grads)


def body(
    tables,
    bag_ids,
    bag_lengths,
    slot_field,
    proj_y,
    proj_p,
    linear_w,
    fm_gain,
    w_up,
    w_down,
    out_gain,
    cotangent,
):
    ids = bag_ids[0].transpose(1, 2, 0)
    lengths = bag_lengths[0].transpose(1, 0)
    slots, up_all, down_all = pool_and_gather(ids, lengths, tables, w_up, w_down)
    layer_out, slot_grads, grads = layer(
        slots,
        slot_field.reshape(1, FIELDS),
        slot_field.reshape(FIELDS, 1),
        proj_y,
        proj_p,
        linear_w,
        fm_gain.reshape(1, E),
        up_all.reshape(TILES, TH, E),
        down_all.reshape(TILES, TH, E),
        out_gain.reshape(1, E),
        cotangent[0],
    )
    bag_grads, grad_up, grad_down = reduce_and_return(slot_grads, grads)
    return (layer_out[None], bag_grads[None], grad_up, grad_down)


def solution(mesh):
    placed = (
        P("emb", None, None),
        P("wide", None, "emb", None),
        P("wide", None, "emb"),
        P(),
        P(),
        P(),
        P(),
        P(),
        P("wide", None),
        P("wide", None),
        P(),
        P("wide", "emb", None, None),
    )
    return jax.shard_map(
        body,
        mesh=mesh,
        in_specs=placed,
        out_specs=(
            P("wide", "emb", None, None),
            P("wide", None, "emb", None),
            P("wide", None),
            P("wide", None),
        ),
        check_vma=False,
    )
```

time: 924 us -> 195 us (0.21)
  waiting for transfers between devices: 715 us -> 0 us
  Pallas kernels: 0 us -> 175 us
  matrix products: 75.6 us -> 0 us
  local copies, waits for them, and re-layouts: 81.1 us -> 16 us
  starting transfers between devices: 21.4 us -> 0 us
  other arithmetic: 14.7 us -> 0 us
  between operations: 14.2 us -> 0.69 us
    reduce_scatter x1 -> x0, waiting for transfers between devices: 315 us -> none  [body(): lax.psum_scatter(jnp.concatenate([up_term, down_term_part], axis=1), 'wid...]
    psum x1 -> x0, waiting for transfers between devices: 265 us -> none  [body(): grad_up, grad_down = lax.psum((up_local, down_local), 'emb')]
    pallas_call x0 -> x3, Pallas kernels: none -> 175 us  [the longest x1 65.7 us: reduce_and_return(): pl.pallas_call(reduce_kernel, name='reduce_and_return', out_shape=(jax.Sh...]
    dot_general x14 -> x0, matrix products: 75.6 us -> none  [the longest x1 13.6 us: body(): jnp.einsum('re,he->rh', grad_ff_rows, down_all, preferred_element_type=jn...]
    all_gather x2 -> x0, waiting for transfers between devices: 72.4 us -> none  [the longest x1 72.4 us: body(): lax.all_gather(w_down, 'wide', axis=0, tiled=True)]
    all_to_all x2 -> x0, waiting for transfers between devices: 61.2 us -> none  [the longest x1 38.5 us: body(): lax.all_to_all(pooled, 'emb', split_axis=1, concat_axis=2, tiled=True)]
    gather x3 -> x0, local copies, waits for them, and re-layouts: 43.9 us -> none  [the longest x2 40.8 us: pool_bags(): jnp.take(tables.reshape(slots_here * bucket_count, -1), flat_ids, axis=0)]
    all_to_all x2 -> x0, starting transfers between devices: 21.3 us -> none  [the longest x1 11.9 us: body(): lax.all_to_all(pooled, 'emb', split_axis=1, concat_axis=2, tiled=True)]
  transfers between devices with their start and end apart: 6 -> 0, of which waited for: 5 -> 0; matrix products, arithmetic and copies ran while one was open for 13% -> 0% of each run, Pallas kernels for 0% -> 0%
where the time goes in v1:
time: 195 us; the launch traced here: 192 us
  Pallas kernels  175 us (90%)
  local copies, waits for them, and re-layouts  16 us (8%)
    pallas_call x1, Pallas kernels, reduce_and_return(): pl.pallas_call(reduce_kernel, name='reduce_and_return', out_shape=(jax.Sh...  65.7 us
    pallas_call x1, Pallas kernels, pool_and_gather(): pl.pallas_call(pool_kernel, name='pool_and_gather', out_shape=(jax.ShapeD...  58.5 us
    pallas_call x1, Pallas kernels, layer(): pl.pallas_call(layer_kernel, name='layer', out_shape=(jax.ShapeDtypeStruc...  50.9 us
    unnamed x24, local copies, waits for them, and re-layouts  14.4 us

profile of v1, /device:TPU:3, one launch (start us, length us, event | category | flops | bytes accessed | tf_op | source)
XLA Modules:
  0.0 191.8 jit_solution(15191980770902142363)
XLA Ops:
  0.6 1.5 copy.16.field_column
  2.2 0.0 copy-start
  2.2 2.2 %copy-done = bf16[16,512,256]{2,1,0:T(8,128)(2,1)S(1)} copy-done((bf16[16,512,256]{2,1,0:T(8,128)(2,1)S(1)}, bf16[16,512,256]{2,1,0:T(8,128)(2,1)}, u32[]{:S(2)}) %copy-start) | copy-done | bytes 4194328
  4.4 0.0 copy-start.5
  4.4 1.0 copy-done.5
  5.4 0.0 copy-start.6
  5.4 1.0 copy-done.6
  6.4 0.0 copy-start.7
  6.4 0.8 copy-done.7
  7.2 0.0 copy-start.8
  7.2 0.7 copy-done.8
  7.9 58.5 %pool_and_gather.1 = (bf16[4,512,256]{2,1,0:T(8,128)(2,1)S(1)}, bf16[4,1024,256]{2,1,0:T(8,128)(2,1)S(1)}, bf16[4,1024,256]{2,1,0:T(8,128)(2,1)S(1)}) custom-call(s32[16,4,128]{2,1,0:T(4,128)S(1)} %bitcast.18, s32[16,128]{1,0:T(8,128)S(1)} %bitcast.19, bf16[16,512,256]{2,1,0:T(8,128)(2,1)S(1)} %copy-done, bf16[1024,256]{1,0:T(8,128)(2,1)S(1)} %copy-done.5, ...), custom_call_target="tpu_custom_call" | custom-call | tf_op jit(solution)/shard_map/pool_and_gather/pallas_call | solution.py:171
  66.4 0.0 copy-start.1
  66.4 1.3 copy-done.1
  67.7 0.0 copy-start.2
  67.7 1.3 copy-done.2
  69.0 0.0 copy-start.4
  69.0 1.0 copy-done.4
  70.0 50.9 %layer.1 = (bf16[4,512,256]{2,1,0:T(8,128)(2,1)}, bf16[4,512,256]{2,1,0:T(8,128)(2,1)}, bf16[2,16,256,256]{3,2,1,0:T(8,128)(2,1)}) custom-call(bf16[4,512,256]{2,1,0:T(8,128)(2,1)} %copy-done.4, s32[1,512]{1,0:T(1,128)} %bitcast.23, s32[512,1]{1,0:T(8,128)} %copy.16.field_column, bf16[512,256]{1,0:T(8,128)(2,1)} %proj_y.1, bf16[128,512]{1,0:T(8,128)(2,1)} %proj_p.1, ...), custom_call_target="tpu_custom_call" | custom-call | tf_op jit(solution)/shard_map/layer/pallas_call | solution.py:347
  120.9 0.0 copy-start.3
  120.9 1.2 copy-done.3
  122.1 0.0 copy-start.9
  122.1 65.7 %reduce_and_return.1 = (bf16[128,16,256]{2,1,0:T(8,128)(2,1)S(1)}, f32[1024,256]{1,0:T(8,128)S(1)}, f32[1024,256]{1,0:T(8,128)S(1)}) custom-call(bf16[4,512,256]{2,1,0:T(8,128)(2,1)S(1)} %copy-done.3, bf16[2,16,256,256]{3,2,1,0:T(8,128)(2,1)} %get-tuple-element.18.grads), custom_call_target="tpu_custom_call" | custom-call | tf_op jit(solution)/shard_map/reduce_and_return/pallas_call | solution.py:552
  187.9 0.0 copy-done.9
  187.9 1.0 copy.21
  188.9 1.0 copy.22
  189.8 1.0 copy.23
  190.8 1.0 copy.24
Async XLA Ops:
  2.2 2.2 %copy-start = (bf16[16,512,256]{2,1,0:T(8,128)(2,1)S(1)}, bf16[16,512,256]{2,1,0:T(8,128)(2,1)}, u32[]{:S(2)}) copy-start(bf16[16,512,256]{2,1,0:T(8,128)(2,1)} %tables.1) | copy-start | bytes 12582916
  4.4 1.0 copy-start.5
  5.4 1.0 copy-start.6
  6.4 0.8 copy-start.7
  7.2 0.7 copy-start.8
  66.4 1.3 copy-start.1
  67.7 1.3 copy-start.2
  69.0 1.0 copy-start.4
  120.9 1.2 copy-start.3
  122.1 65.7 %copy-start.9 = (bf16[4,512,256]{2,1,0:T(8,128)(2,1)S(1)}, bf16[4,512,256]{2,1,0:T(8,128)(2,1)}, u32[]{:S(2)}) copy-start(bf16[4,512,256]{2,1,0:T(8,128)(2,1)} %get-tuple-element.16) | copy-start | bytes 3145732

commit v2 on v0

v2 whole, which is shorter than its diff:
```python
import functools

import jax
import jax.numpy as jnp
from jax import lax
from jax.experimental import pallas as pl
from jax.experimental.pallas import tpu as pltpu
from jax.sharding import PartitionSpec as P

MESH = pl.DeviceIdType.MESH
F32 = jnp.float32
BF16 = jnp.bfloat16

E = 256
FIELDS = 512
ROWS = 512
NF = 128
NL = 384
BAG = 4
SAMPLES = 4
SLOTS = 16
GROUP_B = 128
EMB = 32
XS = 4
YS = 4
ZS = 4
SLICE = 1024
TH = 512
TILES = 8
NROW = SAMPLES * NF
norm_eps = 1e-05


def dot(a, b, ca=1, cb=0):
    return lax.dot_general(a, b, (((ca,), (cb,)), ((), ())), preferred_element_type=F32)


def send(src, dst, send_sem, recv_sem, **device):
    return pltpu.make_async_remote_copy(
        src_ref=src,
        dst_ref=dst,
        send_sem=send_sem,
        recv_sem=recv_sem,
        device_id=device,
        device_id_type=MESH,
    )


def signal(sem, **device):
    pl.semaphore_signal(sem, inc=1, device_id=device, device_id_type=MESH)


def norm_forward(values):
    centre = jnp.mean(values, axis=-1, keepdims=True)
    shifted = values - centre
    scale = lax.rsqrt(jnp.mean(shifted * shifted, axis=-1, keepdims=True) + norm_eps)
    return shifted * scale, scale


def norm_back(unit, scale, gain, upstream):
    scaled = upstream * gain
    return scale * (
        scaled
        - jnp.mean(scaled, axis=-1, keepdims=True)
        - unit * jnp.mean(scaled * unit, axis=-1, keepdims=True)
    )


def layer_kernel(
    ids, lengths, field_row, field_column, fm_gain, out_gain,
    tables, w_up_hbm, w_down_hbm, proj_y_hbm, proj_p_hbm, linear_w_hbm, cotangent_hbm,
    layer_out_hbm, bag_grads, whole,
    pooled, outgoing, slots, w_up, w_down, proj_y, proj_p, linear_w, cotangent, layer_out,
    embeds, crossed, mixing, inter_unit, inter_scale, rows, rows_t, hidden, slope, ff, ff_out, ff_in,
    linear_out, grad_summed, grad_rows, grad_rows_t, grad_lin, norm_out, norm_in,
    slot_grads, grads, from_core, to_x, from_x, to_y, from_y, to_z, from_z,
    table_sem, local_sem, bag_send, bag_recv, back_send, back_recv, w_send, w_recv, pair_send, pair_recv,
    core_send, core_recv, sum_send, sum_recv,
):
    me = lax.axis_index("emb")
    wide = lax.axis_index("wide")
    x = wide // 2
    z_lo = lax.rem(wide, 2)
    partner = wide + 1 - 2 * z_lo
    core = lax.rem(me, 2)
    y = lax.rem(me // 2, YS)
    z = me // (2 * YS)
    sibling = me + 1 - 2 * core

    def x_at(offset):
        return lax.rem(x + XS + offset, XS)

    def wide_at(x_to):
        return x_to * 2 + z_lo

    def emb_at(z_to, y_to):
        return (z_to * YS + y_to) * 2 + core

    def table(s):
        return hidden.at[s // TILES, s % TILES, :, pl.ds(0, E)]

    def fetch(s):
        return pltpu.make_async_copy(tables.at[s], table(s), table_sem.at[s])

    for s in range(SLOTS):
        fetch(s).start()
    staged = [
        pltpu.make_async_copy(src, dst, local_sem.at[n])
        for n, (src, dst) in enumerate(
            (
                (w_up_hbm, w_up.at[x]),
                (w_down_hbm, w_down.at[x]),
                (proj_y_hbm, proj_y),
                (proj_p_hbm, proj_p),
                (linear_w_hbm, linear_w),
                (cotangent_hbm, cotangent),
            )
        )
    ]
    for copy in staged:
        copy.start()

    barrier = pltpu.get_barrier_semaphore()

    @pl.loop(1, EMB)
    def _(k):
        signal(barrier, emb=lax.rem(me + k, EMB))

    for k in range(1, XS):
        signal(barrier, wide=wide_at(x_at(k)))
    signal(barrier, wide=partner)
    pl.semaphore_wait(barrier, EMB - 1 + XS)

    weights = ((w_up_hbm, w_up), (w_down_hbm, w_down))
    for k in range(1, XS):
        for i, (w, full) in enumerate(weights):
            send(w, full.at[x], w_send.at[i, k - 1], w_recv.at[i, k - 1], wide=wide_at(x_at(k))).start()

    def weights_from(k):
        if k == 0:
            staged[0].wait()
            staged[1].wait()
            return
        for i, (w, full) in enumerate(weights):
            copy = send(
                w, full.at[x_at(-k)], w_send.at[i, k - 1], w_recv.at[i, k - 1], wide=wide_at(x_at(-k))
            )
            copy.wait_recv()
            copy.wait_send()

    bucket = lax.broadcasted_iota(jnp.int32, (ROWS, GROUP_B), 0)

    for s in range(SLOTS):
        fetch(s).wait()
        live = lengths[s : s + 1, :]
        counts = jnp.zeros((ROWS, GROUP_B), F32)
        for j in range(BAG):
            wanted = jnp.where(live > j, ids[s, j : j + 1, :], -1)
            counts = counts + jnp.where(bucket == wanted, 1.0, 0.0)
        bags = dot(counts.astype(BF16), table(s)[...], 0, 0)
        for half in range(2):
            pooled[half, pl.ds(s, GROUP_B, stride=SLOTS), :] = bags[:, half * 128 : half * 128 + 128]

    for half in range(2):
        outgoing[:, :, half * 128 : half * 128 + 128] = (
            pooled[half].astype(BF16).reshape(GROUP_B, SLOTS, 128)
        )

    def slots_at(owner):
        return pl.ds(pl.multiple_of(owner * SLOTS, SLOTS), SLOTS)

    def samples_at(owner):
        return pl.ds(owner * SAMPLES, SAMPLES)

    @pl.loop(1, EMB)
    def _(k):
        peer = lax.rem(me + k, EMB)
        send(
            outgoing.at[samples_at(peer)], slots.at[:, slots_at(me), :], bag_send.at[k], bag_recv.at[k], emb=peer
        ).start()

    slots[:, slots_at(me), :] = outgoing[samples_at(me)]

    by_field = jnp.where(
        lax.broadcasted_iota(jnp.int32, (FIELDS, FIELDS), 0) == field_row[...], 1.0, 0.0
    ).astype(BF16)
    for copy in staged[2:]:
        copy.wait()

    @pl.loop(1, EMB)
    def _(k):
        source = lax.rem(me + EMB - k, EMB)
        copy = send(
            outgoing.at[samples_at(source)],
            slots.at[:, slots_at(source), :],
            bag_send.at[k],
            bag_recv.at[k],
            emb=source,
        )
        copy.wait_recv()
        copy.wait_send()

    def exchange(src, dst, n):
        return send(src, dst, pair_send.at[n], pair_recv.at[n], wide=partner)

    def rows_of(b):
        return pl.ds(pl.multiple_of(b * NF, NF), NF)

    def embed(b, _):
        sample = dot(by_field, slots[b]).astype(BF16)
        embeds[b] = sample
        cross = dot(sample, proj_y[...], 0, 0).astype(BF16)
        crossed[b] = cross
        mix = dot(proj_p[...], sample).astype(BF16)
        mixing[b] = mix
        unit, scale = norm_forward(dot(mix, cross))
        inter_unit[b] = unit
        inter_scale[b] = jnp.broadcast_to(scale, (NF, 128))
        rows[0, rows_of(b), :] = (unit * fm_gain[...]).astype(BF16)
        return 0

    lax.fori_loop(0, SAMPLES, embed, 0)
    rows_copy = exchange(rows.at[0], rows.at[1], 0)
    rows_copy.start()
    ff[...] = jnp.zeros_like(ff)

    def forward(group, k):
        chunk = x_at(-k)

        @pl.loop(0, 2)
        def _(t):
            tile = chunk * 2 + t
            here = pl.ds(pl.multiple_of(t * TH, TH), TH)
            gate = dot(rows[group], w_up[chunk, here, :], 1, 1)
            sigma = 0.5 * jnp.tanh(0.5 * gate) + 0.5
            act = gate * sigma
            slope[group, tile] = (sigma + act * (1.0 - sigma)).astype(BF16)
            act = act.astype(BF16)
            hidden[group, tile] = act
            ff[group] += dot(act, w_down[chunk, here, :])

    weights_from(0)
    forward(0, 0)

    def linear(b, _):
        linear_out[b] = dot(linear_w[...], embeds[b])
        return 0

    lax.fori_loop(0, SAMPLES, linear, 0)
    rows_copy.wait()
    forward(1, 0)
    for k in range(1, XS):
        weights_from(k)
        forward(1, k)
    ff_out[...] = ff[1].astype(BF16)
    ff_copy = exchange(ff_out, ff_in, 1)
    ff_copy.start()
    for k in range(1, XS):
        forward(0, k)
    rows_t[0] = rows[0].astype(F32).T.astype(BF16)
    rows_t[1] = rows[1].astype(F32).T.astype(BF16)
    ff_copy.wait()

    def finish(values, b, first, count):
        here = slice(first, first + count)
        unit, scale = norm_forward(values + embeds[b, here, :].astype(F32))
        layer_out[b, here, :] = (unit * out_gain[...]).astype(BF16)
        grad = norm_back(unit, scale, out_gain[...], cotangent[b, here, :].astype(F32))
        grad_summed[b, here, :] = grad
        return grad.astype(BF16)

    def finish_ff(b, _):
        total = ff[0, rows_of(b), :] + ff_in[rows_of(b), :].astype(F32)
        grad_rows[0, rows_of(b), :] = finish(total, b, 0, NF)
        return 0

    lax.fori_loop(0, SAMPLES, finish_ff, 0)
    grad_copy = exchange(grad_rows.at[0], grad_rows.at[1], 2)
    grad_copy.start()

    def finish_linear(b, _):
        grad_lin[b] = finish(linear_out[b], b, NF, NL)
        grad_summed[b] += dot(linear_w[...], grad_lin[b], 0, 0)
        return 0

    lax.fori_loop(0, SAMPLES, finish_linear, 0)
    layer_copy = pltpu.make_async_copy(layer_out, layer_out_hbm, local_sem.at[6])
    layer_copy.start()
    grad_rows_t[0] = grad_rows[0].astype(F32).T.astype(BF16)
    ff[...] = jnp.zeros_like(ff)
    grad_copy.wait()
    grad_rows_t[1] = grad_rows[1].astype(F32).T.astype(BF16)

    def gate_back(group, chunk, t):
        here = pl.ds(pl.multiple_of(t * TH, TH), TH)
        tile = chunk * 2 + t
        grad_hidden = dot(grad_rows[group], w_down[chunk, here, :], 1, 1)
        grad_gate = (grad_hidden * slope[group, tile].astype(F32)).astype(BF16)
        ff[group] += dot(grad_gate, w_up[chunk, here, :])
        return grad_gate

    @pl.loop(0, TILES)
    def _(tile):
        slope[1, tile] = gate_back(1, tile // 2, lax.rem(tile, 2))

    norm_out[...] = ff[1].astype(BF16)
    norm_copy = exchange(norm_out, norm_in, 3)
    norm_copy.start()

    def over_cores(k):
        chunk = pl.ds(x_at(k) * 4, 4)
        return send(
            grads.at[1 - core, chunk], from_core.at[chunk], core_send.at[k], core_recv.at[k], emb=sibling
        )

    def over_x(k):
        return send(
            to_x.at[pl.ds(x_at(k) * 4, 4)],
            from_x.at[k - 1],
            sum_send.at[k],
            sum_recv.at[k],
            wide=wide_at(x_at(k)),
        )

    def pass_on(k):
        over_cores(k).wait()

        @pl.loop(0, 4)
        def _(t):
            part = x_at(k) * 4 + t
            to_x[part] = (grads[core, part].astype(F32) + from_core[part].astype(F32)).astype(BF16)

        over_x(k).start()

    order = (1, 2, 3, 0)
    for n, k in enumerate(order):
        chunk = x_at(k)

        @pl.loop(0, 2)
        def _(t):
            tile = chunk * 2 + t
            grad_gate = gate_back(0, chunk, t)
            up = dot(rows_t[0], grad_gate) + dot(rows_t[1], slope[1, tile])
            down = dot(grad_rows_t[0], hidden[0, tile]) + dot(grad_rows_t[1], hidden[1, tile])
            for kind, part in enumerate((up, down)):
                part = part.astype(BF16)
                for half in range(2):
                    grads[kind, tile * 2 + half] = part[:, half * 256 : half * 256 + 256]

        over_cores(k).start()
        if n:
            pass_on(order[n - 1])

    norm_copy.wait()

    by_slot = jnp.where(
        lax.broadcasted_iota(jnp.int32, (FIELDS, FIELDS), 1) == field_column[...], 1.0, 0.0
    ).astype(BF16)

    def tail(b, _):
        upstream = ff[0, rows_of(b), :] + norm_in[rows_of(b), :].astype(F32)
        grad_inter = norm_back(inter_unit[b], inter_scale[b, :, 0:1], fm_gain[...], upstream).astype(BF16)
        grad_mixing = dot(grad_inter, crossed[b], 1, 1).astype(BF16)
        grad_crossed = dot(mixing[b], grad_inter, 0, 0).astype(BF16)
        total = grad_summed[b] + dot(proj_p[...], grad_mixing, 0, 0)
        total = total + dot(proj_y[...], grad_crossed, 1, 1)
        slot_grads[b] = dot(by_slot, total.astype(BF16)).astype(BF16)
        return 0

    lax.fori_loop(0, SAMPLES, tail, 0)

    @pl.loop(1, EMB)
    def _(k):
        peer = lax.rem(me + k, EMB)
        send(
            slot_grads.at[:, slots_at(peer), :],
            bag_grads.at[samples_at(me)],
            back_send.at[k],
            back_recv.at[k],
            emb=peer,
        ).start()

    own_bags = pltpu.make_async_copy(
        slot_grads.at[:, slots_at(me), :], bag_grads.at[samples_at(me)], local_sem.at[7]
    )
    own_bags.start()

    over_cores(0).wait()
    for k in range(1, XS):
        over_x(k).wait()

    @pl.loop(0, 4)
    def _(t):
        mine = x * 4 + t
        total = grads[core, mine].astype(F32) + from_core[mine].astype(F32)
        for k in range(XS - 1):
            total = total + from_x[k, t].astype(F32)
        to_y[t] = total.astype(BF16)

    def over_y(k):
        peer = lax.rem(y + k, YS)
        return send(
            to_y.at[peer], from_y.at[k - 1], sum_send.at[3 + k], sum_recv.at[3 + k], emb=emb_at(z, peer)
        )

    for k in range(1, YS):
        over_y(k).start()
    for k in range(1, YS):
        over_y(k).wait()

    total = to_y[y].astype(F32)
    for k in range(YS - 1):
        total = total + from_y[k].astype(F32)
    for part in range(ZS):
        to_z[part] = total[
            (part % 2) * 128 : (part % 2) * 128 + 128, (part // 2) * 128 : (part // 2) * 128 + 128
        ].astype(BF16)

    def over_z(k):
        peer = lax.rem(z + k, ZS)
        return send(
            to_z.at[peer], from_z.at[k - 1], sum_send.at[6 + k], sum_recv.at[6 + k], emb=emb_at(peer, y)
        )

    for k in range(1, ZS):
        over_z(k).start()
    for k in range(1, ZS):
        over_z(k).wait()

    total = to_z[z].astype(F32)
    for k in range(ZS - 1):
        total = total + from_z[k].astype(F32)

    def piece(z_of):
        row = pl.multiple_of(y * 256 + (z_of // 2) * 128, 128)
        column = pl.multiple_of(lax.rem(z_of, 2) * 128, 128)
        return whole.at[core, pl.ds(row, 128), pl.ds(column, 128)]

    row = pl.multiple_of(y * 256 + (z // 2) * 128, 128)
    column = pl.multiple_of(lax.rem(z, 2) * 128, 128)
    whole[core, pl.ds(row, 128), pl.ds(column, 128)] = total.T.astype(BF16)

    def spread(src, dst, n, peer):
        return send(src, dst, sum_send.at[n], sum_recv.at[n], emb=peer)

    for k in range(1, ZS):
        spread(piece(z), piece(z), 9 + k, emb_at(lax.rem(z + k, ZS), y)).start()
    for k in range(1, ZS):
        source = lax.rem(z + ZS - k, ZS)
        spread(piece(z), piece(source), 9 + k, emb_at(source, y)).wait()

    def band(y_of):
        return whole.at[core, pl.ds(pl.multiple_of(y_of * 256, 256), 256), :]

    for k in range(1, YS):
        spread(band(y), band(y), 12 + k, emb_at(z, lax.rem(y + k, YS))).start()
    for k in range(1, YS):
        source = lax.rem(y + YS - k, YS)
        spread(band(y), band(source), 12 + k, emb_at(z, source)).wait()

    spread(whole.at[core], whole.at[core], 16, sibling).start()
    spread(whole.at[core], whole.at[1 - core], 16, sibling).wait()

    @pl.loop(1, EMB)
    def _(k):
        source = lax.rem(me + EMB - k, EMB)
        copy = send(
            slot_grads.at[:, slots_at(source), :],
            bag_grads.at[samples_at(source)],
            back_send.at[k],
            back_recv.at[k],
            emb=source,
        )
        copy.wait_recv()
        copy.wait_send()

    own_bags.wait()
    layer_copy.wait()


def whole_layer(*operands):
    anywhere = pl.BlockSpec(memory_space=pl.ANY)
    vmem = pl.BlockSpec(memory_space=pltpu.VMEM)
    dma = pltpu.SemaphoreType.DMA
    return pl.pallas_call(
        layer_kernel,
        name="whole_layer",
        out_shape=(
            jax.ShapeDtypeStruct((SAMPLES, FIELDS, E), BF16),
            jax.ShapeDtypeStruct((GROUP_B, SLOTS, E), BF16),
            jax.ShapeDtypeStruct((2, SLICE, E), BF16),
        ),
        in_specs=[vmem] * 6 + [anywhere] * 7,
        out_specs=(anywhere, anywhere, vmem),
        scratch_shapes=[
            pltpu.VMEM((2, GROUP_B * SLOTS, 128), F32),
            pltpu.VMEM((GROUP_B, SLOTS, E), BF16),
            pltpu.VMEM((SAMPLES, FIELDS, E), BF16),
            pltpu.VMEM((XS, SLICE, E), BF16),
            pltpu.VMEM((XS, SLICE, E), BF16),
            pltpu.VMEM((FIELDS, E), BF16),
            pltpu.VMEM((NF, FIELDS), BF16),
            pltpu.VMEM((NL, FIELDS), BF16),
            pltpu.VMEM((SAMPLES, FIELDS, E), BF16),
            pltpu.VMEM((SAMPLES, FIELDS, E), BF16),
            pltpu.VMEM((SAMPLES, FIELDS, E), BF16),
            pltpu.VMEM((SAMPLES, E, E), BF16),
            pltpu.VMEM((SAMPLES, NF, E), BF16),
            pltpu.VMEM((SAMPLES, NF, E), F32),
            pltpu.VMEM((SAMPLES, NF, 128), F32),
            pltpu.VMEM((2, NROW, E), BF16),
            pltpu.VMEM((2, E, NROW), BF16),
            pltpu.VMEM((2, TILES, NROW, TH), BF16),
            pltpu.VMEM((2, TILES, NROW, TH), BF16),
            pltpu.VMEM((2, NROW, E), F32),
            pltpu.VMEM((NROW, E), BF16),
            pltpu.VMEM((NROW, E), BF16),
            pltpu.VMEM((SAMPLES, NL, E), F32),
            pltpu.VMEM((SAMPLES, FIELDS, E), F32),
            pltpu.VMEM((2, NROW, E), BF16),
            pltpu.VMEM((2, E, NROW), BF16),
            pltpu.VMEM((SAMPLES, NL, E), BF16),
            pltpu.VMEM((NROW, E), BF16),
            pltpu.VMEM((NROW, E), BF16),
            pltpu.VMEM((SAMPLES, FIELDS, E), BF16),
            pltpu.VMEM((2, TILES * 2, 256, 256), BF16),
            pltpu.VMEM((TILES * 2, 256, 256), BF16),
            pltpu.VMEM((TILES * 2, 256, 256), BF16),
            pltpu.VMEM((XS - 1, 4, 256, 256), BF16),
            pltpu.VMEM((YS, 256, 256), BF16),
            pltpu.VMEM((YS - 1, 256, 256), BF16),
            pltpu.VMEM((ZS, 128, 128), BF16),
            pltpu.VMEM((ZS - 1, 128, 128), BF16),
            dma((SLOTS,)),
            dma((8,)),
            dma((EMB,)),
            dma((EMB,)),
            dma((EMB,)),
            dma((EMB,)),
            dma((2, XS - 1)),
            dma((2, XS - 1)),
            dma((4,)),
            dma((4,)),
            dma((XS,)),
            dma((XS,)),
            dma((17,)),
            dma((17,)),
        ],
        compiler_params=pltpu.CompilerParams(
            collective_id=0, has_side_effects=True, vmem_limit_bytes=62 << 20
        ),
    )(*operands)


def body(
    tables,
    bag_ids,
    bag_lengths,
    slot_field,
    proj_y,
    proj_p,
    linear_w,
    fm_gain,
    w_up,
    w_down,
    out_gain,
    cotangent,
):
    layer_out, bag_grads, weight_grads = whole_layer(
        bag_ids[0].transpose(1, 2, 0),
        bag_lengths[0].transpose(1, 0),
        slot_field.reshape(1, FIELDS),
        slot_field.reshape(FIELDS, 1),
        fm_gain.reshape(1, E),
        out_gain.reshape(1, E),
        tables,
        w_up,
        w_down,
        proj_y,
        proj_p,
        linear_w,
        cotangent[0],
    )
    return (
        layer_out[None],
        bag_grads[None],
        weight_grads[0].astype(F32),
        weight_grads[1].astype(F32),
    )


def solution(mesh):
    placed = (
        P("emb", None, None),
        P("wide", None, "emb", None),
        P("wide", None, "emb"),
        P(),
        P(),
        P(),
        P(),
        P(),
        P("wide", None),
        P("wide", None),
        P(),
        P("wide", "emb", None, None),
    )
    return jax.shard_map(
        body,
        mesh=mesh,
        in_specs=placed,
        out_specs=(
            P("wide", "emb", None, None),
            P("wide", None, "emb", None),
            P("wide", None),
            P("wide", None),
        ),
        check_vma=False,
    )
```

time: 924 us -> 156 us (0.17)
  waiting for transfers between devices: 715 us -> 0 us
  Pallas kernels: 0 us -> 147 us
  local copies, waits for them, and re-layouts: 81.1 us -> 4.77 us
  matrix products: 75.6 us -> 0 us
  starting transfers between devices: 21.4 us -> 0 us
  between operations: 14.2 us -> 0.65 us
  other arithmetic: 14.7 us -> 2.77 us
    reduce_scatter x1 -> x0, waiting for transfers between devices: 315 us -> none  [body(): lax.psum_scatter(jnp.concatenate([up_term, down_term_part], axis=1), 'wid...]
    psum x1 -> x0, waiting for transfers between devices: 265 us -> none  [body(): grad_up, grad_down = lax.psum((up_local, down_local), 'emb')]
    pallas_call x0 -> x1, Pallas kernels: none -> 147 us  [whole_layer(): pl.pallas_call(layer_kernel, name='whole_layer', out_shape=(jax.ShapeDtyp...]
    dot_general x14 -> x0, matrix products: 75.6 us -> none  [the longest x1 13.6 us: body(): jnp.einsum('re,he->rh', grad_ff_rows, down_all, preferred_element_type=jn...]
    all_gather x2 -> x0, waiting for transfers between devices: 72.4 us -> none  [the longest x1 72.4 us: body(): lax.all_gather(w_down, 'wide', axis=0, tiled=True)]
    all_to_all x2 -> x0, waiting for transfers between devices: 61.2 us -> none  [the longest x1 38.5 us: body(): lax.all_to_all(pooled, 'emb', split_axis=1, concat_axis=2, tiled=True)]
    gather x3 -> x0, local copies, waits for them, and re-layouts: 43.9 us -> none  [the longest x2 40.8 us: pool_bags(): jnp.take(tables.reshape(slots_here * bucket_count, -1), flat_ids, axis=0)]
    all_to_all x2 -> x0, starting transfers between devices: 21.3 us -> none  [the longest x1 11.9 us: body(): lax.all_to_all(pooled, 'emb', split_axis=1, concat_axis=2, tiled=True)]
  transfers between devices with their start and end apart: 6 -> 0, of which waited for: 5 -> 0; matrix products, arithmetic and copies ran while one was open for 13% -> 0% of each run, Pallas kernels for 0% -> 0%
where the time goes in v2:
time: 156 us; the launch traced here: 155 us
  Pallas kernels  147 us (94%)
  local copies, waits for them, and re-layouts  4.77 us (3%)
  other arithmetic  2.77 us (2%)
    pallas_call x1, Pallas kernels, whole_layer(): pl.pallas_call(layer_kernel, name='whole_layer', out_shape=(jax.ShapeDtyp...  147 us
    unnamed x4, local copies, waits for them, and re-layouts  3.24 us

profile of v2, /device:TPU:3, one launch (start us, length us, event | category | flops | bytes accessed | tf_op | source)
XLA Modules:
  0.0 155.3 jit_solution(12283313390239326105)
XLA Ops:
  0.6 1.5 copy.16.field_column
  2.2 147.1 %whole_layer.1 = (bf16[4,512,256]{2,1,0:T(8,128)(2,1)}, bf16[128,16,256]{2,1,0:T(8,128)(2,1)}, bf16[2,1024,256]{2,1,0:T(8,128)(2,1)}) custom-call(s32[16,4,128]{2,1,0:T(4,128)} %bitcast.22, s32[16,128]{1,0:T(8,128)} %bitcast.23, s32[1,512]{1,0:T(1,128)} %bitcast.25, s32[512,1]{1,0:T(8,128)} %copy.16.field_column, f32[1,256]{1,0:T(1,128)} %bitcast.26, ...), custom_call_target="tpu_custom_call" | custom-call | tf_op jit(solution)/shard_map/whole_layer/pallas_call | solution.py:485
  149.3 0.0 copy-start
  149.3 2.8 %bitcast_convert_fusion = (f32[1024,256]{1,0:T(8,128)}, f32[1024,256]{1,0:T(8,128)}) fusion(bf16[2,1024,256]{2,1,0:T(8,128)(2,1)} %get-tuple-element.9), kind=kLoop, calls=%fused_computation | loop fusion | flops 524288 | bytes 3145728 | tf_op jit(solution)/shard_map/convert_element_type | solution.py:588
  152.1 2.3 %copy.19 = bf16[1,4,512,256]{3,2,1,0:T(8,128)(2,1)} copy(bf16[1,4,512,256]{3,2,1,0:T(8,128)(2,1)} %bitcast.20) | data formatting | bytes 2097152
  154.4 0.0 copy-done
  154.4 1.0 copy.20
Async XLA Ops:
  149.3 5.0 %copy-start = (bf16[128,16,256]{2,1,0:T(8,128)(2,1)S(1)}, bf16[128,16,256]{2,1,0:T(8,128)(2,1)}, u32[]{:S(2)}) copy-start(bf16[128,16,256]{2,1,0:T(8,128)(2,1)} %get-tuple-element.8) | copy-start | bytes 3145732

commit v3 on v2

--- a/solution.py
+++ b/solution.py
@@ -67,13 +67,13 @@
 
 
 def layer_kernel(
-    ids, lengths, field_row, field_column, fm_gain, out_gain,
+    ids, lengths, field_row, fm_gain, out_gain,
     tables, w_up_hbm, w_down_hbm, proj_y_hbm, proj_p_hbm, linear_w_hbm, cotangent_hbm,
     layer_out_hbm, bag_grads, whole,
     pooled, outgoing, slots, w_up, w_down, proj_y, proj_p, linear_w, cotangent, layer_out,
     embeds, crossed, mixing, inter_unit, inter_scale, rows, rows_t, hidden, slope, ff, ff_out, ff_in,
-    linear_out, grad_summed, grad_rows, grad_rows_t, grad_lin, norm_out, norm_in,
-    slot_grads, grads, from_core, to_x, from_x, to_y, from_y, to_z, from_z,
+    by_slot, linear_out, grad_summed, grad_rows, grad_rows_t, grad_lin, norm_out, norm_in,
+    slot_grads, grads, from_core, to_x, from_x, to_y, from_y, to_z, from_z, done_z,
     table_sem, local_sem, bag_send, bag_recv, back_send, back_recv, w_send, w_recv, pair_send, pair_recv,
     core_send, core_recv, sum_send, sum_recv,
 ):
@@ -131,10 +131,19 @@
     signal(barrier, wide=partner)
     pl.semaphore_wait(barrier, EMB - 1 + XS)
 
+    def half_of(which):
+        return pl.ds(pl.multiple_of(which * TH, TH), TH)
+
     weights = ((w_up_hbm, w_up), (w_down_hbm, w_down))
     for k in range(1, XS):
         for i, (w, full) in enumerate(weights):
-            send(w, full.at[x], w_send.at[i, k - 1], w_recv.at[i, k - 1], wide=wide_at(x_at(k))).start()
+            send(
+                w.at[half_of(core)],
+                full.at[x, half_of(core)],
+                w_send.at[i, k - 1],
+                w_recv.at[i, k - 1],
+                wide=wide_at(x_at(k)),
+            ).start()
 
     def weights_from(k):
         if k == 0:
@@ -142,11 +151,12 @@
             staged[1].wait()
             return
         for i, (w, full) in enumerate(weights):
-            copy = send(
-                w, full.at[x_at(-k)], w_send.at[i, k - 1], w_recv.at[i, k - 1], wide=wide_at(x_at(-k))
-            )
-            copy.wait_recv()
-            copy.wait_send()
+            pass_weights(i, k, 1 - core).wait_recv()
+            pass_weights(i, k, core).wait_send()
+
+    def pass_weights(i, k, which):
+        part = weights[i][1].at[x_at(-k), half_of(which)]
+        return send(part, part, w_send.at[2 + i, k - 1], w_recv.at[2 + i, k - 1], emb=sibling)
 
     bucket = lax.broadcasted_iota(jnp.int32, (ROWS, GROUP_B), 0)
 
@@ -184,8 +194,22 @@
     by_field = jnp.where(
         lax.broadcasted_iota(jnp.int32, (FIELDS, FIELDS), 0) == field_row[...], 1.0, 0.0
     ).astype(BF16)
+    by_slot[...] = by_field.astype(F32).T.astype(BF16)
     for copy in staged[2:]:
         copy.wait()
+
+    for k in (1, 3, 2):
+        for i, (w, full) in enumerate(weights):
+            copy = send(
+                w.at[half_of(core)],
+                full.at[x_at(-k), half_of(core)],
+                w_send.at[i, k - 1],
+                w_recv.at[i, k - 1],
+                wide=wide_at(x_at(-k)),
+            )
+            copy.wait_recv()
+            copy.wait_send()
+            pass_weights(i, k, core).start()
 
     @pl.loop(1, EMB)
     def _(k):
@@ -299,63 +323,177 @@
         ff[group] += dot(grad_gate, w_up[chunk, here, :])
         return grad_gate
 
-    @pl.loop(0, TILES)
-    def _(tile):
-        slope[1, tile] = gate_back(1, tile // 2, lax.rem(tile, 2))
+    k_mine = pl.ds(pl.multiple_of(core * 128, 128), 128)
+    k_other = pl.ds(pl.multiple_of(128 - core * 128, 128), 128)
+
+    def keep(kind, tile, part):
+        part = part.astype(BF16)
+        for half in range(2):
+            grads[kind, tile * 2 + half] = part[:, half * 256 : half * 256 + 256]
+
+    def over_cores(kind, k):
+        chunk = pl.ds(x_at(k) * 4, 4)
+        return send(
+            grads.at[kind, chunk, k_other],
+            from_core.at[kind, chunk],
+            core_send.at[kind, k],
+            core_recv.at[kind, k],
+            emb=sibling,
+        )
+
+    def over_x(kind, k):
+        return send(
+            to_x.at[kind, pl.ds(x_at(k) * 4, 4)],
+            from_x.at[kind, k - 1],
+            sum_send.at[kind, k],
+            sum_recv.at[kind, k],
+            wide=wide_at(x_at(k)),
+        )
+
+    def over_y(kind, k):
+        peer = lax.rem(y + k, YS)
+        return send(
+            to_y.at[kind, peer],
+            from_y.at[kind, k - 1],
+            sum_send.at[kind, 3 + k],
+            sum_recv.at[kind, 3 + k],
+            emb=emb_at(z, peer),
+        )
+
+    def over_z(kind, k):
+        peer = lax.rem(z + k, ZS)
+        return send(
+            to_z.at[kind, peer],
+            from_z.at[kind, k - 1],
+            sum_send.at[kind, 6 + k],
+            sum_recv.at[kind, 6 + k],
+            emb=emb_at(peer, y),
+        )
+
+    def along_z(kind, k, z_of, z_to):
+        part = done_z.at[kind, z_of]
+        return send(part, part, sum_send.at[kind, 9 + k], sum_recv.at[kind, 9 + k], emb=emb_at(z_to, y))
+
+    def band(kind, y_of, columns):
+        return whole.at[kind, pl.ds(pl.multiple_of(y_of * 256, 256), 256), columns]
+
+    def along_y(kind, k, y_of, y_to):
+        part = band(kind, y_of, k_mine)
+        return send(part, part, sum_send.at[kind, 12 + k], sum_recv.at[kind, 12 + k], emb=emb_at(z, y_to))
+
+    def to_sibling(kind, k, columns):
+        part = band(kind, lax.rem(y + YS - k, YS), columns)
+        return send(part, part, sum_send.at[kind, 16 + k], sum_recv.at[kind, 16 + k], emb=sibling)
+
+    def pass_on(kind, k):
+        over_cores(kind, k).wait()
+
+        @pl.loop(0, 4)
+        def _(t):
+            part = x_at(k) * 4 + t
+            to_x[kind, part] = (
+                grads[kind, part, k_mine].astype(F32) + from_core[kind, part].astype(F32)
+            ).astype(BF16)
+
+        over_x(kind, k).start()
+
+    def sum_x(kind):
+        over_cores(kind, 0).wait()
+        for k in range(1, XS):
+            over_x(kind, k).wait()
+
+        @pl.loop(0, 4)
+        def _(t):
+            mine = x * 4 + t
+            total = grads[kind, mine, k_mine].astype(F32) + from_core[kind, mine].astype(F32)
+            for k in range(XS - 1):
+                total = total + from_x[kind, k, t].astype(F32)
+            to_y[kind, t] = total.astype(BF16)
+
+        for k in range(1, YS):
+            over_y(kind, k).start()
+
+    def sum_y(kind):
+        for k in range(1, YS):
+            over_y(kind, k).wait()
+        total = to_y[kind, y].astype(F32)
+        for k in range(YS - 1):
+            total = total + from_y[kind, k].astype(F32)
+        to_z[kind] = total.astype(BF16).reshape(ZS, 128 // ZS, 256)
+        for k in range(1, ZS):
+            over_z(kind, k).start()
+
+    def sum_z(kind):
+        for k in range(1, ZS):
+            over_z(kind, k).wait()
+        total = to_z[kind, z].astype(F32)
+        for k in range(ZS - 1):
+            total = total + from_z[kind, k].astype(F32)
+        done_z[kind, z] = total.astype(BF16)
+        for k in range(1, ZS):
+            along_z(kind, k, z, lax.rem(z + k, ZS)).start()
+
+    def spread_y(kind):
+        for k in range(1, ZS):
+            source = lax.rem(z + ZS - k, ZS)
+            along_z(kind, k, z, source).wait_send()
+            along_z(kind, k, source, source).wait_recv()
+        part = done_z[kind].reshape(128, 256).astype(F32).T.astype(BF16)
+        whole[kind, pl.ds(pl.multiple_of(y * 256, 256), 256), k_mine] = part
+        for k in range(1, YS):
+            along_y(kind, k, y, lax.rem(y + k, YS)).start()
+        to_sibling(kind, 0, k_mine).start()
+
+    def spread_cores(kind):
+        for k in range(1, YS):
+            source = lax.rem(y + YS - k, YS)
+            along_y(kind, k, source, source).wait_recv()
+            to_sibling(kind, k, k_mine).start()
+
+    def settle(kind):
+        for k in range(1, YS):
+            along_y(kind, k, y, lax.rem(y + k, YS)).wait_send()
+        for k in range(YS):
+            to_sibling(kind, k, k_mine).wait_send()
+            to_sibling(kind, k, k_other).wait_recv()
+
+    order = (1, 2, 3, 0)
+    for k in order:
+
+        @pl.loop(0, 2)
+        def _(t):
+            tile = x_at(k) * 2 + t
+            keep(1, tile, dot(grad_rows_t[0], hidden[0, tile]) + dot(grad_rows_t[1], hidden[1, tile]))
+
+        over_cores(1, k).start()
+
+    for n, k in enumerate(order):
+
+        @pl.loop(0, 2)
+        def _(t):
+            slope[1, x_at(k) * 2 + t] = gate_back(1, x_at(k), t)
+
+        if n < 3:
+            pass_on(1, k)
 
     norm_out[...] = ff[1].astype(BF16)
     norm_copy = exchange(norm_out, norm_in, 3)
     norm_copy.start()
 
-    def over_cores(k):
-        chunk = pl.ds(x_at(k) * 4, 4)
-        return send(
-            grads.at[1 - core, chunk], from_core.at[chunk], core_send.at[k], core_recv.at[k], emb=sibling
-        )
-
-    def over_x(k):
-        return send(
-            to_x.at[pl.ds(x_at(k) * 4, 4)],
-            from_x.at[k - 1],
-            sum_send.at[k],
-            sum_recv.at[k],
-            wide=wide_at(x_at(k)),
-        )
-
-    def pass_on(k):
-        over_cores(k).wait()
-
-        @pl.loop(0, 4)
-        def _(t):
-            part = x_at(k) * 4 + t
-            to_x[part] = (grads[core, part].astype(F32) + from_core[part].astype(F32)).astype(BF16)
-
-        over_x(k).start()
-
-    order = (1, 2, 3, 0)
     for n, k in enumerate(order):
-        chunk = x_at(k)
 
         @pl.loop(0, 2)
         def _(t):
-            tile = chunk * 2 + t
-            grad_gate = gate_back(0, chunk, t)
-            up = dot(rows_t[0], grad_gate) + dot(rows_t[1], slope[1, tile])
-            down = dot(grad_rows_t[0], hidden[0, tile]) + dot(grad_rows_t[1], hidden[1, tile])
-            for kind, part in enumerate((up, down)):
-                part = part.astype(BF16)
-                for half in range(2):
-                    grads[kind, tile * 2 + half] = part[:, half * 256 : half * 256 + 256]
-
-        over_cores(k).start()
+            tile = x_at(k) * 2 + t
+            grad_gate = gate_back(0, x_at(k), t)
+            keep(0, tile, dot(rows_t[0], grad_gate) + dot(rows_t[1], slope[1, tile]))
+
+        over_cores(0, k).start()
         if n:
-            pass_on(order[n - 1])
+            pass_on(0, order[n - 1])
+        (lambda kind: None, sum_x, sum_y, sum_z)[n](1)
 
     norm_copy.wait()
-
-    by_slot = jnp.where(
-        lax.broadcasted_iota(jnp.int32, (FIELDS, FIELDS), 1) == field_column[...], 1.0, 0.0
-    ).astype(BF16)
 
     def tail(b, _):
         upstream = ff[0, rows_of(b), :] + norm_in[rows_of(b), :].astype(F32)
@@ -364,7 +502,7 @@
         grad_crossed = dot(mixing[b], grad_inter, 0, 0).astype(BF16)
         total = grad_summed[b] + dot(proj_p[...], grad_mixing, 0, 0)
         total = total + dot(proj_y[...], grad_crossed, 1, 1)
-        slot_grads[b] = dot(by_slot, total.astype(BF16)).astype(BF16)
+        slot_grads[b] = dot(by_slot[...], total.astype(BF16)).astype(BF16)
         return 0
 
     lax.fori_loop(0, SAMPLES, tail, 0)
@@ -385,81 +523,15 @@
     )
     own_bags.start()
 
-    over_cores(0).wait()
-    for k in range(1, XS):
-        over_x(k).wait()
-
-    @pl.loop(0, 4)
-    def _(t):
-        mine = x * 4 + t
-        total = grads[core, mine].astype(F32) + from_core[mine].astype(F32)
-        for k in range(XS - 1):
-            total = total + from_x[k, t].astype(F32)
-        to_y[t] = total.astype(BF16)
-
-    def over_y(k):
-        peer = lax.rem(y + k, YS)
-        return send(
-            to_y.at[peer], from_y.at[k - 1], sum_send.at[3 + k], sum_recv.at[3 + k], emb=emb_at(z, peer)
-        )
-
-    for k in range(1, YS):
-        over_y(k).start()
-    for k in range(1, YS):
-        over_y(k).wait()
-
-    total = to_y[y].astype(F32)
-    for k in range(YS - 1):
-        total = total + from_y[k].astype(F32)
-    for part in range(ZS):
-        to_z[part] = total[
-            (part % 2) * 128 : (part % 2) * 128 + 128, (part // 2) * 128 : (part // 2) * 128 + 128
-        ].astype(BF16)
-
-    def over_z(k):
-        peer = lax.rem(z + k, ZS)
-        return send(
-            to_z.at[peer], from_z.at[k - 1], sum_send.at[6 + k], sum_recv.at[6 + k], emb=emb_at(peer, y)
-        )
-
-    for k in range(1, ZS):
-        over_z(k).start()
-    for k in range(1, ZS):
-        over_z(k).wait()
-
-    total = to_z[z].astype(F32)
-    for k in range(ZS - 1):
-        total = total + from_z[k].astype(F32)
-
-    def piece(z_of):
-        row = pl.multiple_of(y * 256 + (z_of // 2) * 128, 128)
-        column = pl.multiple_of(lax.rem(z_of, 2) * 128, 128)
-        return whole.at[core, pl.ds(row, 128), pl.ds(column, 128)]
-
-    row = pl.multiple_of(y * 256 + (z // 2) * 128, 128)
-    column = pl.multiple_of(lax.rem(z, 2) * 128, 128)
-    whole[core, pl.ds(row, 128), pl.ds(column, 128)] = total.T.astype(BF16)
-
-    def spread(src, dst, n, peer):
-        return send(src, dst, sum_send.at[n], sum_recv.at[n], emb=peer)
-
-    for k in range(1, ZS):
-        spread(piece(z), piece(z), 9 + k, emb_at(lax.rem(z + k, ZS), y)).start()
-    for k in range(1, ZS):
-        source = lax.rem(z + ZS - k, ZS)
-        spread(piece(z), piece(source), 9 + k, emb_at(source, y)).wait()
-
-    def band(y_of):
-        return whole.at[core, pl.ds(pl.multiple_of(y_of * 256, 256), 256), :]
-
-    for k in range(1, YS):
-        spread(band(y), band(y), 12 + k, emb_at(z, lax.rem(y + k, YS))).start()
-    for k in range(1, YS):
-        source = lax.rem(y + YS - k, YS)
-        spread(band(y), band(source), 12 + k, emb_at(z, source)).wait()
-
-    spread(whole.at[core], whole.at[core], 16, sibling).start()
-    spread(whole.at[core], whole.at[1 - core], 16, sibling).wait()
+    spread_y(1)
+    sum_x(0)
+    spread_cores(1)
+    sum_y(0)
+    sum_z(0)
+    spread_y(0)
+    spread_cores(0)
+    settle(1)
+    settle(0)
 
     @pl.loop(1, EMB)
     def _(k):
@@ -490,7 +562,7 @@
             jax.ShapeDtypeStruct((GROUP_B, SLOTS, E), BF16),
             jax.ShapeDtypeStruct((2, SLICE, E), BF16),
         ),
-        in_specs=[vmem] * 6 + [anywhere] * 7,
+        in_specs=[vmem] * 5 + [anywhere] * 7,
         out_specs=(anywhere, anywhere, vmem),
         scratch_shapes=[
             pltpu.VMEM((2, GROUP_B * SLOTS, 128), F32),
@@ -515,6 +587,7 @@
             pltpu.VMEM((2, NROW, E), F32),
             pltpu.VMEM((NROW, E), BF16),
             pltpu.VMEM((NROW, E), BF16),
+            pltpu.VMEM((FIELDS, FIELDS), BF16),
             pltpu.VMEM((SAMPLES, NL, E), F32),
             pltpu.VMEM((SAMPLES, FIELDS, E), F32),
             pltpu.VMEM((2, NROW, E), BF16),
@@ -524,32 +597,69 @@
             pltpu.VMEM((NROW, E), BF16),
             pltpu.VMEM((SAMPLES, FIELDS, E), BF16),
             pltpu.VMEM((2, TILES * 2, 256, 256), BF16),
-            pltpu.VMEM((TILES * 2, 256, 256), BF16),
-            pltpu.VMEM((TILES * 2, 256, 256), BF16),
-            pltpu.VMEM((XS - 1, 4, 256, 256), BF16),
-            pltpu.VMEM((YS, 256, 256), BF16),
-            pltpu.VMEM((YS - 1, 256, 256), BF16),
-            pltpu.VMEM((ZS, 128, 128), BF16),
-            pltpu.VMEM((ZS - 1, 128, 128), BF16),
+            pltpu.VMEM((2, TILES * 2, 128, 256), BF16),
+            pltpu.VMEM((2, TILES * 2, 128, 256), BF16),
+            pltpu.VMEM((2, XS - 1, 4, 128, 256), BF16),
+            pltpu.VMEM((2, YS, 128, 256), BF16),
+            pltpu.VMEM((2, YS - 1, 128, 256), BF16),
+            pltpu.VMEM((2, ZS, 128 // ZS, 256), BF16),
+            pltpu.VMEM((2, ZS - 1, 128 // ZS, 256), BF16),
+            pltpu.VMEM((2, ZS, 128 // ZS, 256), BF16),
             dma((SLOTS,)),
             dma((8,)),
             dma((EMB,)),
             dma((EMB,)),
             dma((EMB,)),
             dma((EMB,)),
-            dma((2, XS - 1)),
-            dma((2, XS - 1)),
+            dma((4, XS - 1)),
+            dma((4, XS - 1)),
             dma((4,)),
             dma((4,)),
-            dma((XS,)),
-            dma((XS,)),
-            dma((17,)),
-            dma((17,)),
+            dma((2, XS)),
+            dma((2, XS)),
+            dma((2, 20)),
+            dma((2, 20)),
         ],
         compiler_params=pltpu.CompilerParams(
             collective_id=0, has_side_effects=True, vmem_limit_bytes=62 << 20
         ),
     )(*operands)
+
+
+def finish_kernel(layer_out, bag_grads, whole, layer_final, bag_final, up, down, up_held, down_held, sem):
+    first = pltpu.make_async_copy(layer_out, layer_final, sem.at[0])
+    second = pltpu.make_async_copy(bag_grads, bag_final, sem.at[1])
+    first.start()
+    second.start()
+    up_held[...] = whole[0].astype(F32)
+    up_copy = pltpu.make_async_copy(up_held, up, sem.at[2])
+    up_copy.start()
+    down_held[...] = whole[1].astype(F32)
+    down_copy = pltpu.make_async_copy(down_held, down, sem.at[3])
+    down_copy.start()
+    for copy in (first, second, up_copy, down_copy):
+        copy.wait()
+
+
+def finish_outputs(layer_out, bag_grads, whole):
+    anywhere = pl.BlockSpec(memory_space=pl.ANY)
+    return pl.pallas_call(
+        finish_kernel,
+        name="finish_outputs",
+        out_shape=(
+            jax.ShapeDtypeStruct(layer_out.shape, BF16),
+            jax.ShapeDtypeStruct(bag_grads.shape, BF16),
+            jax.ShapeDtypeStruct((SLICE, E), F32),
+            jax.ShapeDtypeStruct((SLICE, E), F32),
+        ),
+        in_specs=[anywhere, anywhere, pl.BlockSpec(memory_space=pltpu.VMEM)],
+        out_specs=(anywhere,) * 4,
+        scratch_shapes=[
+            pltpu.VMEM((SLICE, E), F32),
+            pltpu.VMEM((SLICE, E), F32),
+            pltpu.SemaphoreType.DMA((4,)),
+        ],
+    )(layer_out, bag_grads, whole)
 
 
 def body(
@@ -570,7 +680,6 @@
         bag_ids[0].transpose(1, 2, 0),
         bag_lengths[0].transpose(1, 0),
         slot_field.reshape(1, FIELDS),
-        slot_field.reshape(FIELDS, 1),
         fm_gain.reshape(1, E),
         out_gain.reshape(1, E),
         tables,
@@ -581,12 +690,8 @@
         linear_w,
         cotangent[0],
     )
-    return (
-        layer_out[None],
-        bag_grads[None],
-        weight_grads[0].astype(F32),
-        weight_grads[1].astype(F32),
-    )
+    layer_out, bag_grads, grad_up, grad_down = finish_outputs(layer_out, bag_grads, weight_grads)
+    return (layer_out[None], bag_grads[None], grad_up, grad_down)
 
 
 def solution(mesh):

time: 156 us -> 217 us (1.39)
  Pallas kernels: 147 us -> 216 us
  local copies, waits for them, and re-layouts: 4.77 us -> 0 us
  other arithmetic: 2.77 us -> 0 us
    pallas_call x0 -> x1, Pallas kernels: none -> 65.9 us  [finish_outputs(): pl.pallas_call(finish_kernel, name='finish_outputs', out_shape=(jax.Shape...]
    unnamed x4 -> x0, local copies, waits for them, and re-layouts: 3.24 us -> none
    convert_element_type x1 -> x0, other arithmetic: 2.77 us -> none  [body(): weight_grads[1].astype(F32)]
    pallas_call x1, Pallas kernels: 147 us -> 150 us  [whole_layer(): pl.pallas_call(layer_kernel, name='whole_layer', out_shape=(jax.ShapeDtyp...]
where the time goes in v3:
time: 217 us; the launch traced here: 216 us
  Pallas kernels  216 us (100%)
    pallas_call x1, Pallas kernels, whole_layer(): pl.pallas_call(layer_kernel, name='whole_layer', out_shape=(jax.ShapeDtyp...  150 us
    pallas_call x1, Pallas kernels, finish_outputs(): pl.pallas_call(finish_kernel, name='finish_outputs', out_shape=(jax.Shape...  65.9 us

profile of v3, /device:TPU:3, one launch (start us, length us, event | category | flops | bytes accessed | tf_op | source)
XLA Modules:
  0.0 216.4 jit_solution(13777199427434900430)
XLA Ops:
  0.6 149.7 %whole_layer.1 = (bf16[4,512,256]{2,1,0:T(8,128)(2,1)}, bf16[128,16,256]{2,1,0:T(8,128)(2,1)}, bf16[2,1024,256]{2,1,0:T(8,128)(2,1)}) custom-call(s32[16,4,128]{2,1,0:T(4,128)} %bitcast.13, s32[16,128]{1,0:T(8,128)} %bitcast.14, s32[1,512]{1,0:T(1,128)} %bitcast.15, f32[1,256]{1,0:T(1,128)} %bitcast.16, f32[1,256]{1,0:T(1,128)} %bitcast.17, ...), custom_call_target="tpu_custom_call" | custom-call | tf_op jit(solution)/shard_map/whole_layer/pallas_call | solution.py:557
  150.4 65.9 %finish_outputs.1 = (bf16[4,512,256]{2,1,0:T(8,128)(2,1)}, bf16[128,16,256]{2,1,0:T(8,128)(2,1)}, f32[1024,256]{1,0:T(8,128)}, f32[1024,256]{1,0:T(8,128)}) custom-call(bf16[4,512,256]{2,1,0:T(8,128)(2,1)} %get-tuple-element.11.layer_out, bf16[128,16,256]{2,1,0:T(8,128)(2,1)} %get-tuple-element.12.bag_grads, bf16[2,1024,256]{2,1,0:T(8,128)(2,1)} %get-tuple-element.13.whole), custom_call_target="tpu_custom_call" | custom-call | tf_op jit(solution)/shard_map/finish_outputs/pallas_call | solution.py:646

commit v4 on v3

--- a/solution.py
+++ b/solution.py
@@ -24,6 +24,8 @@
 XS = 4
 YS = 4
 ZS = 4
+PIECES = YS * ZS
+PIECE = 32
 SLICE = 1024
 TH = 512
 TILES = 8
@@ -69,13 +71,13 @@
 def layer_kernel(
     ids, lengths, field_row, fm_gain, out_gain,
     tables, w_up_hbm, w_down_hbm, proj_y_hbm, proj_p_hbm, linear_w_hbm, cotangent_hbm,
-    layer_out_hbm, bag_grads, whole,
+    layer_out_hbm, bag_grads, done,
     pooled, outgoing, slots, w_up, w_down, proj_y, proj_p, linear_w, cotangent, layer_out,
     embeds, crossed, mixing, inter_unit, inter_scale, rows, rows_t, hidden, slope, ff, ff_out, ff_in,
     by_slot, linear_out, grad_summed, grad_rows, grad_rows_t, grad_lin, norm_out, norm_in,
-    slot_grads, grads, from_core, to_x, from_x, to_y, from_y, to_z, from_z, done_z,
+    slot_grads, grads, from_core, to_x, from_x, to_piece, from_piece,
     table_sem, local_sem, bag_send, bag_recv, back_send, back_recv, w_send, w_recv, pair_send, pair_recv,
-    core_send, core_recv, sum_send, sum_recv,
+    core_send, core_recv, sum_send, sum_recv, piece_send, piece_recv, done_send, done_recv, last_send, last_recv,
 ):
     me = lax.axis_index("emb")
     wide = lax.axis_index("wide")
@@ -93,8 +95,13 @@
     def wide_at(x_to):
         return x_to * 2 + z_lo
 
-    def emb_at(z_to, y_to):
-        return (z_to * YS + y_to) * 2 + core
+    piece = y * ZS + z
+
+    def piece_at(offset):
+        return lax.rem(piece + PIECES + offset, PIECES)
+
+    def owner(of):
+        return (lax.rem(of, ZS) * YS + of // ZS) * 2 + core
 
     def table(s):
         return hidden.at[s // TILES, s % TILES, :, pl.ds(0, E)]
@@ -350,40 +357,23 @@
             wide=wide_at(x_at(k)),
         )
 
-    def over_y(kind, k):
-        peer = lax.rem(y + k, YS)
+    def over_pieces(kind, k):
+        peer = piece_at(k)
         return send(
-            to_y.at[kind, peer],
-            from_y.at[kind, k - 1],
-            sum_send.at[kind, 3 + k],
-            sum_recv.at[kind, 3 + k],
-            emb=emb_at(z, peer),
+            to_piece.at[kind, peer],
+            from_piece.at[kind, k],
+            piece_send.at[kind, k],
+            piece_recv.at[kind, k],
+            emb=owner(peer),
         )
 
-    def over_z(kind, k):
-        peer = lax.rem(z + k, ZS)
-        return send(
-            to_z.at[kind, peer],
-            from_z.at[kind, k - 1],
-            sum_send.at[kind, 6 + k],
-            sum_recv.at[kind, 6 + k],
-            emb=emb_at(peer, y),
-        )
-
-    def along_z(kind, k, z_of, z_to):
-        part = done_z.at[kind, z_of]
-        return send(part, part, sum_send.at[kind, 9 + k], sum_recv.at[kind, 9 + k], emb=emb_at(z_to, y))
-
-    def band(kind, y_of, columns):
-        return whole.at[kind, pl.ds(pl.multiple_of(y_of * 256, 256), 256), columns]
-
-    def along_y(kind, k, y_of, y_to):
-        part = band(kind, y_of, k_mine)
-        return send(part, part, sum_send.at[kind, 12 + k], sum_recv.at[kind, 12 + k], emb=emb_at(z, y_to))
-
-    def to_sibling(kind, k, columns):
-        part = band(kind, lax.rem(y + YS - k, YS), columns)
-        return send(part, part, sum_send.at[kind, 16 + k], sum_recv.at[kind, 16 + k], emb=sibling)
+    def spread(kind, k, of, to):
+        part = done.at[kind, core, of]
+        return send(part, part, done_send.at[kind, k], done_recv.at[kind, k], emb=owner(to))
+
+    def to_sibling(kind, k, half):
+        part = done.at[kind, half, piece_at(-k)]
+        return send(part, part, last_send.at[kind, k], last_recv.at[kind, k], emb=sibling)
 
     def pass_on(kind, k):
         over_cores(kind, k).wait()
@@ -408,54 +398,43 @@
             total = grads[kind, mine, k_mine].astype(F32) + from_core[kind, mine].astype(F32)
             for k in range(XS - 1):
                 total = total + from_x[kind, k, t].astype(F32)
-            to_y[kind, t] = total.astype(BF16)
-
-        for k in range(1, YS):
-            over_y(kind, k).start()
-
-    def sum_y(kind):
-        for k in range(1, YS):
-            over_y(kind, k).wait()
-        total = to_y[kind, y].astype(F32)
-        for k in range(YS - 1):
-            total = total + from_y[kind, k].astype(F32)
-        to_z[kind] = total.astype(BF16).reshape(ZS, 128 // ZS, 256)
-        for k in range(1, ZS):
-            over_z(kind, k).start()
-
-    def sum_z(kind):
-        for k in range(1, ZS):
-            over_z(kind, k).wait()
-        total = to_z[kind, z].astype(F32)
-        for k in range(ZS - 1):
-            total = total + from_z[kind, k].astype(F32)
-        done_z[kind, z] = total.astype(BF16)
-        for k in range(1, ZS):
-            along_z(kind, k, z, lax.rem(z + k, ZS)).start()
-
-    def spread_y(kind):
-        for k in range(1, ZS):
-            source = lax.rem(z + ZS - k, ZS)
-            along_z(kind, k, z, source).wait_send()
-            along_z(kind, k, source, source).wait_recv()
-        part = done_z[kind].reshape(128, 256).astype(F32).T.astype(BF16)
-        whole[kind, pl.ds(pl.multiple_of(y * 256, 256), 256), k_mine] = part
-        for k in range(1, YS):
-            along_y(kind, k, y, lax.rem(y + k, YS)).start()
-        to_sibling(kind, 0, k_mine).start()
-
-    def spread_cores(kind):
-        for k in range(1, YS):
-            source = lax.rem(y + YS - k, YS)
-            along_y(kind, k, source, source).wait_recv()
-            to_sibling(kind, k, k_mine).start()
+            to_piece[kind, pl.ds(t * ZS, ZS)] = total.astype(BF16).reshape(ZS, PIECE, 256)
+
+        @pl.loop(1, PIECES)
+        def _(k):
+            over_pieces(kind, k).start()
+
+    def sum_pieces(kind):
+        @pl.loop(1, PIECES)
+        def _(k):
+            over_pieces(kind, k).wait()
+
+        total = to_piece[kind, piece].astype(F32)
+        for k in range(1, PIECES):
+            total = total + from_piece[kind, k].astype(F32)
+        done[kind, core, piece] = total.astype(BF16)
+
+        @pl.loop(1, PIECES)
+        def _(k):
+            spread(kind, k, piece, piece_at(k)).start()
+
+        to_sibling(kind, 0, core).start()
+
+    def hand_over(kind):
+        @pl.loop(1, PIECES)
+        def _(k):
+            spread(kind, k, piece_at(-k), piece_at(-k)).wait_recv()
+            to_sibling(kind, k, core).start()
 
     def settle(kind):
-        for k in range(1, YS):
-            along_y(kind, k, y, lax.rem(y + k, YS)).wait_send()
-        for k in range(YS):
-            to_sibling(kind, k, k_mine).wait_send()
-            to_sibling(kind, k, k_other).wait_recv()
+        @pl.loop(1, PIECES)
+        def _(k):
+            spread(kind, k, piece, piece_at(k)).wait_send()
+
+        @pl.loop(0, PIECES)
+        def _(k):
+            to_sibling(kind, k, core).wait_send()
+            to_sibling(kind, k, 1 - core).wait_recv()
 
     order = (1, 2, 3, 0)
     for k in order:
@@ -491,7 +470,7 @@
         over_cores(0, k).start()
         if n:
             pass_on(0, order[n - 1])
-        (lambda kind: None, sum_x, sum_y, sum_z)[n](1)
+        (lambda kind: None, lambda kind: None, sum_x, sum_pieces)[n](1)
 
     norm_copy.wait()
 
@@ -523,13 +502,10 @@
     )
     own_bags.start()
 
-    spread_y(1)
+    hand_over(1)
     sum_x(0)
-    spread_cores(1)
-    sum_y(0)
-    sum_z(0)
-    spread_y(0)
-    spread_cores(0)
+    sum_pieces(0)
+    hand_over(0)
     settle(1)
     settle(0)
 
@@ -560,7 +536,7 @@
         out_shape=(
             jax.ShapeDtypeStruct((SAMPLES, FIELDS, E), BF16),
             jax.ShapeDtypeStruct((GROUP_B, SLOTS, E), BF16),
-            jax.ShapeDtypeStruct((2, SLICE, E), BF16),
+            jax.ShapeDtypeStruct((2, 2, PIECES, PIECE, 256), BF16),
         ),
         in_specs=[vmem] * 5 + [anywhere] * 7,
         out_specs=(anywhere, anywhere, vmem),
@@ -600,11 +576,8 @@
             pltpu.VMEM((2, TILES * 2, 128, 256), BF16),
             pltpu.VMEM((2, TILES * 2, 128, 256), BF16),
             pltpu.VMEM((2, XS - 1, 4, 128, 256), BF16),
-            pltpu.VMEM((2, YS, 128, 256), BF16),
-            pltpu.VMEM((2, YS - 1, 128, 256), BF16),
-            pltpu.VMEM((2, ZS, 128 // ZS, 256), BF16),
-            pltpu.VMEM((2, ZS - 1, 128 // ZS, 256), BF16),
-            pltpu.VMEM((2, ZS, 128 // ZS, 256), BF16),
+            pltpu.VMEM((2, PIECES, PIECE, 256), BF16),
+            pltpu.VMEM((2, PIECES, PIECE, 256), BF16),
             dma((SLOTS,)),
             dma((8,)),
             dma((EMB,)),
@@ -617,8 +590,14 @@
             dma((4,)),
             dma((2, XS)),
             dma((2, XS)),
-            dma((2, 20)),
-            dma((2, 20)),
+            dma((2, XS)),
+            dma((2, XS)),
+            dma((2, PIECES)),
+            dma((2, PIECES)),
+            dma((2, PIECES)),
+            dma((2, PIECES)),
+            dma((2, PIECES)),
+            dma((2, PIECES)),
         ],
         compiler_params=pltpu.CompilerParams(
             collective_id=0, has_side_effects=True, vmem_limit_bytes=62 << 20
@@ -626,23 +605,39 @@
     )(*operands)
 
 
-def finish_kernel(layer_out, bag_grads, whole, layer_final, bag_final, up, down, up_held, down_held, sem):
-    first = pltpu.make_async_copy(layer_out, layer_final, sem.at[0])
-    second = pltpu.make_async_copy(bag_grads, bag_final, sem.at[1])
-    first.start()
-    second.start()
-    up_held[...] = whole[0].astype(F32)
-    up_copy = pltpu.make_async_copy(up_held, up, sem.at[2])
-    up_copy.start()
-    down_held[...] = whole[1].astype(F32)
-    down_copy = pltpu.make_async_copy(down_held, down, sem.at[3])
-    down_copy.start()
-    for copy in (first, second, up_copy, down_copy):
+def finish_kernel(layer_out, bag_grads, done, layer_final, bag_final, up, down, held, sums, in_sem, out_sem, sum_sem):
+    pairs = ((layer_out, layer_final), (bag_grads, bag_final))
+    rows = [layer_out.shape[0] // 2, bag_grads.shape[0] // 2]
+    incoming, outgoing = [], []
+    for n, (src, dst) in enumerate(pairs):
+        for half in range(2):
+            part = pl.ds(half * rows[n], rows[n])
+            here = held[n].at[part]
+            incoming.append(pltpu.make_async_copy(src.at[part], here, in_sem.at[n, half]))
+            outgoing.append(pltpu.make_async_copy(here, dst.at[part], out_sem.at[n, half]))
+    for copy in incoming:
+        copy.start()
+    sum_copies = []
+    for kind, out in enumerate((up, down)):
+        for y in range(YS):
+            part = pl.ds(y * 256, 256)
+            for half in range(2):
+                block = done[kind, half, y * ZS : y * ZS + ZS].reshape(128, 256)
+                sums[kind, part, half * 128 : half * 128 + 128] = block.astype(F32).T
+            copy = pltpu.make_async_copy(sums.at[kind, part], out.at[part], sum_sem.at[kind, y])
+            copy.start()
+            sum_copies.append(copy)
+            n = kind * YS + y
+            if n % 2 == 1:
+                incoming[n // 2].wait()
+                outgoing[n // 2].start()
+    for copy in outgoing + sum_copies:
         copy.wait()
 
 
-def finish_outputs(layer_out, bag_grads, whole):
+def finish_outputs(layer_out, bag_grads, done):
     anywhere = pl.BlockSpec(memory_space=pl.ANY)
+    dma = pltpu.SemaphoreType.DMA
     return pl.pallas_call(
         finish_kernel,
         name="finish_outputs",
@@ -655,11 +650,13 @@
         in_specs=[anywhere, anywhere, pl.BlockSpec(memory_space=pltpu.VMEM)],
         out_specs=(anywhere,) * 4,
         scratch_shapes=[
-            pltpu.VMEM((SLICE, E), F32),
-            pltpu.VMEM((SLICE, E), F32),
-            pltpu.SemaphoreType.DMA((4,)),
+            [pltpu.VMEM(layer_out.shape, BF16), pltpu.VMEM(bag_grads.shape, BF16)],
+            pltpu.VMEM((2, SLICE, E), F32),
+            dma((2, 2)),
+            dma((2, 2)),
+            dma((2, YS)),
         ],
-    )(layer_out, bag_grads, whole)
+    )(layer_out, bag_grads, done)
 
 
 def body(
@@ -676,7 +673,7 @@
     out_gain,
     cotangent,
 ):
-    layer_out, bag_grads, weight_grads = whole_layer(
+    layer_out, bag_grads, done = whole_layer(
         bag_ids[0].transpose(1, 2, 0),
         bag_lengths[0].transpose(1, 0),
         slot_field.reshape(1, FIELDS),
@@ -690,7 +687,7 @@
         linear_w,
         cotangent[0],
     )
-    layer_out, bag_grads, grad_up, grad_down = finish_outputs(layer_out, bag_grads, weight_grads)
+    layer_out, bag_grads, grad_up, grad_down = finish_outputs(layer_out, bag_grads, done)
     return (layer_out[None], bag_grads[None], grad_up, grad_down)
 
 

time: 217 us -> 163 us (0.75)
  Pallas kernels: 216 us -> 162 us
    pallas_call x1, Pallas kernels: 65.9 us -> 4.34 us  [finish_outputs(): pl.pallas_call(finish_kernel, name='finish_outputs', out_shape=(jax.Shape...]
    pallas_call x1, Pallas kernels: 150 us -> 157 us  [whole_layer(): pl.pallas_call(layer_kernel, name='whole_layer', out_shape=(jax.ShapeDtyp...]
where the time goes in v4:
time: 163 us; the launch traced here: 162 us
  Pallas kernels  162 us (99%)
    pallas_call x1, Pallas kernels, whole_layer(): pl.pallas_call(layer_kernel, name='whole_layer', out_shape=(jax.ShapeDtyp...  157 us
    pallas_call x1, Pallas kernels, finish_outputs(): pl.pallas_call(finish_kernel, name='finish_outputs', out_shape=(jax.Shape...  4.34 us

profile of v4, /device:TPU:3, one launch (start us, length us, event | category | flops | bytes accessed | tf_op | source)
XLA Modules:
  0.0 162.5 jit_solution(500698363283502054)
XLA Ops:
  0.6 157.3 %whole_layer.1 = (bf16[4,512,256]{2,1,0:T(8,128)(2,1)}, bf16[128,16,256]{2,1,0:T(8,128)(2,1)}, bf16[2,2,16,32,256]{4,3,2,1,0:T(8,128)(2,1)}) custom-call(s32[16,4,128]{2,1,0:T(4,128)} %bitcast.13, s32[16,128]{1,0:T(8,128)} %bitcast.14, s32[1,512]{1,0:T(1,128)} %bitcast.15, f32[1,256]{1,0:T(1,128)} %bitcast.16, f32[1,256]{1,0:T(1,128)} %bitcast.17, ...), custom_call_target="tpu_custom_call" | custom-call | tf_op jit(solution)/shard_map/whole_layer/pallas_call | solution.py:533
  158.0 4.3 %finish_outputs.1 = (bf16[4,512,256]{2,1,0:T(8,128)(2,1)}, bf16[128,16,256]{2,1,0:T(8,128)(2,1)}, f32[1024,256]{1,0:T(8,128)}, f32[1024,256]{1,0:T(8,128)}) custom-call(bf16[4,512,256]{2,1,0:T(8,128)(2,1)} %get-tuple-element.11.layer_out, bf16[128,16,256]{2,1,0:T(8,128)(2,1)} %get-tuple-element.12.bag_grads, bf16[2,2,16,32,256]{4,3,2,1,0:T(8,128)(2,1)} %get-tuple-element.13.done), custom_call_target="tpu_custom_call" | custom-call | tf_op jit(solution)/shard_map/finish_outputs/pallas_call | solution.py:641

commit v5 on v3

--- a/solution.py
+++ b/solution.py
@@ -129,22 +129,10 @@
     for k in range(1, XS):
         signal(barrier, wide=wide_at(x_at(k)))
     signal(barrier, wide=partner)
-    pl.semaphore_wait(barrier, EMB - 1 + XS)
-
     def half_of(which):
         return pl.ds(pl.multiple_of(which * TH, TH), TH)
 
     weights = ((w_up_hbm, w_up), (w_down_hbm, w_down))
-    for k in range(1, XS):
-        for i, (w, full) in enumerate(weights):
-            send(
-                w.at[half_of(core)],
-                full.at[x, half_of(core)],
-                w_send.at[i, k - 1],
-                w_recv.at[i, k - 1],
-                wide=wide_at(x_at(k)),
-            ).start()
-
     def weights_from(k):
         if k == 0:
             staged[0].wait()
@@ -161,6 +149,17 @@
     bucket = lax.broadcasted_iota(jnp.int32, (ROWS, GROUP_B), 0)
 
     for s in range(SLOTS):
+        if s == SLOTS // 2:
+            pl.semaphore_wait(barrier, EMB - 1 + XS)
+            for k in range(1, XS):
+                for i, (w, full) in enumerate(weights):
+                    send(
+                        w.at[half_of(core)],
+                        full.at[x, half_of(core)],
+                        w_send.at[i, k - 1],
+                        w_recv.at[i, k - 1],
+                        wide=wide_at(x_at(k)),
+                    ).start()
         fetch(s).wait()
         live = lengths[s : s + 1, :]
         counts = jnp.zeros((ROWS, GROUP_B), F32)
@@ -491,9 +490,11 @@
         over_cores(0, k).start()
         if n:
             pass_on(0, order[n - 1])
-        (lambda kind: None, sum_x, sum_y, sum_z)[n](1)
+        if n == 2:
+            sum_x(1)
 
     norm_copy.wait()
+    sum_y(1)
 
     def tail(b, _):
         upstream = ff[0, rows_of(b), :] + norm_in[rows_of(b), :].astype(F32)
@@ -507,27 +508,33 @@
 
     lax.fori_loop(0, SAMPLES, tail, 0)
 
-    @pl.loop(1, EMB)
-    def _(k):
-        peer = lax.rem(me + k, EMB)
-        send(
-            slot_grads.at[:, slots_at(peer), :],
-            bag_grads.at[samples_at(me)],
-            back_send.at[k],
-            back_recv.at[k],
-            emb=peer,
-        ).start()
-
+    sum_z(1)
+
+    def bags_back(first, last):
+        @pl.loop(first, last)
+        def _(k):
+            peer = lax.rem(me + k, EMB)
+            send(
+                slot_grads.at[:, slots_at(peer), :],
+                bag_grads.at[samples_at(me)],
+                back_send.at[k],
+                back_recv.at[k],
+                emb=peer,
+            ).start()
+
+    bags_back(1, 8)
     own_bags = pltpu.make_async_copy(
         slot_grads.at[:, slots_at(me), :], bag_grads.at[samples_at(me)], local_sem.at[7]
     )
     own_bags.start()
-
+    sum_x(0)
+    bags_back(8, 16)
     spread_y(1)
-    sum_x(0)
+    sum_y(0)
+    bags_back(16, 24)
+    sum_z(0)
+    bags_back(24, EMB)
     spread_cores(1)
-    sum_y(0)
-    sum_z(0)
     spread_y(0)
     spread_cores(0)
     settle(1)
@@ -626,23 +633,37 @@
     )(*operands)
 
 
-def finish_kernel(layer_out, bag_grads, whole, layer_final, bag_final, up, down, up_held, down_held, sem):
-    first = pltpu.make_async_copy(layer_out, layer_final, sem.at[0])
-    second = pltpu.make_async_copy(bag_grads, bag_final, sem.at[1])
-    first.start()
-    second.start()
-    up_held[...] = whole[0].astype(F32)
-    up_copy = pltpu.make_async_copy(up_held, up, sem.at[2])
-    up_copy.start()
-    down_held[...] = whole[1].astype(F32)
-    down_copy = pltpu.make_async_copy(down_held, down, sem.at[3])
-    down_copy.start()
-    for copy in (first, second, up_copy, down_copy):
+def finish_kernel(layer_out, bag_grads, whole, layer_final, bag_final, up, down, held, sums, in_sem, out_sem, sum_sem):
+    pairs = ((layer_out, layer_final), (bag_grads, bag_final))
+    rows = [layer_out.shape[0] // 2, bag_grads.shape[0] // 2]
+    incoming, outgoing = [], []
+    for n, (src, dst) in enumerate(pairs):
+        for half in range(2):
+            part = pl.ds(half * rows[n], rows[n])
+            here = held[n].at[part]
+            incoming.append(pltpu.make_async_copy(src.at[part], here, in_sem.at[n, half]))
+            outgoing.append(pltpu.make_async_copy(here, dst.at[part], out_sem.at[n, half]))
+    for copy in incoming:
+        copy.start()
+    sum_copies = []
+    for kind, out in enumerate((up, down)):
+        for y in range(YS):
+            part = pl.ds(y * 256, 256)
+            sums[kind, part] = whole[kind, part].astype(F32)
+            copy = pltpu.make_async_copy(sums.at[kind, part], out.at[part], sum_sem.at[kind, y])
+            copy.start()
+            sum_copies.append(copy)
+            n = kind * YS + y
+            if n % 2 == 1:
+                incoming[n // 2].wait()
+                outgoing[n // 2].start()
+    for copy in outgoing + sum_copies:
         copy.wait()
 
 
 def finish_outputs(layer_out, bag_grads, whole):
     anywhere = pl.BlockSpec(memory_space=pl.ANY)
+    dma = pltpu.SemaphoreType.DMA
     return pl.pallas_call(
         finish_kernel,
         name="finish_outputs",
@@ -655,9 +676,11 @@
         in_specs=[anywhere, anywhere, pl.BlockSpec(memory_space=pltpu.VMEM)],
         out_specs=(anywhere,) * 4,
         scratch_shapes=[
-            pltpu.VMEM((SLICE, E), F32),
-            pltpu.VMEM((SLICE, E), F32),
-            pltpu.SemaphoreType.DMA((4,)),
+            [pltpu.VMEM(layer_out.shape, BF16), pltpu.VMEM(bag_grads.shape, BF16)],
+            pltpu.VMEM((2, SLICE, E), F32),
+            dma((2, 2)),
+            dma((2, 2)),
+            dma((2, YS)),
         ],
     )(layer_out, bag_grads, whole)
 

time: 217 us -> 152 us (0.70)
  Pallas kernels: 216 us -> 150 us
    pallas_call x1, Pallas kernels: 65.9 us -> 4.43 us  [finish_outputs(): pl.pallas_call(finish_kernel, name='finish_outputs', out_shape=(jax.Shape...]
    pallas_call x1, Pallas kernels: 150 us -> 146 us  [whole_layer(): pl.pallas_call(layer_kernel, name='whole_layer', out_shape=(jax.ShapeDtyp...]
where the time goes in v5:
time: 152 us; the launch traced here: 151 us
  Pallas kernels  150 us (99%)
    pallas_call x1, Pallas kernels, whole_layer(): pl.pallas_call(layer_kernel, name='whole_layer', out_shape=(jax.ShapeDtyp...  146 us
    pallas_call x1, Pallas kernels, finish_outputs(): pl.pallas_call(finish_kernel, name='finish_outputs', out_shape=(jax.Shape...  4.43 us

profile of v5, /device:TPU:3, one launch (start us, length us, event | category | flops | bytes accessed | tf_op | source)
XLA Modules:
  0.0 151.2 jit_solution(3468415364210072078)
XLA Ops:
  0.6 146.0 %whole_layer.1 = (bf16[4,512,256]{2,1,0:T(8,128)(2,1)}, bf16[128,16,256]{2,1,0:T(8,128)(2,1)}, bf16[2,1024,256]{2,1,0:T(8,128)(2,1)}) custom-call(s32[16,4,128]{2,1,0:T(4,128)} %bitcast.13, s32[16,128]{1,0:T(8,128)} %bitcast.14, s32[1,512]{1,0:T(1,128)} %bitcast.15, f32[1,256]{1,0:T(1,128)} %bitcast.16, f32[1,256]{1,0:T(1,128)} %bitcast.17, ...), custom_call_target="tpu_custom_call" | custom-call | tf_op jit(solution)/shard_map/whole_layer/pallas_call | solution.py:564
  146.6 4.4 %finish_outputs.1 = (bf16[4,512,256]{2,1,0:T(8,128)(2,1)}, bf16[128,16,256]{2,1,0:T(8,128)(2,1)}, f32[1024,256]{1,0:T(8,128)}, f32[1024,256]{1,0:T(8,128)}) custom-call(bf16[4,512,256]{2,1,0:T(8,128)(2,1)} %get-tuple-element.11.layer_out, bf16[128,16,256]{2,1,0:T(8,128)(2,1)} %get-tuple-element.12.bag_grads, bf16[2,1024,256]{2,1,0:T(8,128)(2,1)} %get-tuple-element.13.whole), custom_call_target="tpu_custom_call" | custom-call | tf_op jit(solution)/shard_map/finish_outputs/pallas_call | solution.py:667

commit v6 on v5

--- a/solution.py
+++ b/solution.py
@@ -466,35 +466,38 @@
 
         over_cores(1, k).start()
 
-    for n, k in enumerate(order):
-
+    def both_back(k, t):
+        tile = x_at(k) * 2 + t
+        theirs = gate_back(1, x_at(k), t)
+        mine = gate_back(0, x_at(k), t)
+        keep(0, tile, dot(rows_t[0], mine) + dot(rows_t[1], theirs))
+
+    def chunk_back(k):
         @pl.loop(0, 2)
         def _(t):
-            slope[1, x_at(k) * 2 + t] = gate_back(1, x_at(k), t)
-
-        if n < 3:
-            pass_on(1, k)
-
+            both_back(k, t)
+
+        over_cores(0, k).start()
+
+    pass_on(1, 1)
+    pass_on(1, 2)
+    chunk_back(1)
+    pass_on(1, 3)
+    chunk_back(2)
+    pass_on(0, 1)
+    chunk_back(3)
+    pass_on(0, 2)
+    both_back(0, 0)
+    pass_on(0, 3)
+    sum_x(1)
+    both_back(0, 1)
+    over_cores(0, 0).start()
     norm_out[...] = ff[1].astype(BF16)
     norm_copy = exchange(norm_out, norm_in, 3)
     norm_copy.start()
-
-    for n, k in enumerate(order):
-
-        @pl.loop(0, 2)
-        def _(t):
-            tile = x_at(k) * 2 + t
-            grad_gate = gate_back(0, x_at(k), t)
-            keep(0, tile, dot(rows_t[0], grad_gate) + dot(rows_t[1], slope[1, tile]))
-
-        over_cores(0, k).start()
-        if n:
-            pass_on(0, order[n - 1])
-        if n == 2:
-            sum_x(1)
-
+    sum_y(1)
+    sum_x(0)
     norm_copy.wait()
-    sum_y(1)
 
     def tail(b, _):
         upstream = ff[0, rows_of(b), :] + norm_in[rows_of(b), :].astype(F32)
@@ -506,9 +509,10 @@
         slot_grads[b] = dot(by_slot[...], total.astype(BF16)).astype(BF16)
         return 0
 
-    lax.fori_loop(0, SAMPLES, tail, 0)
-
+    lax.fori_loop(0, SAMPLES // 2, tail, 0)
     sum_z(1)
+    sum_y(0)
+    lax.fori_loop(SAMPLES // 2, SAMPLES, tail, 0)
 
     def bags_back(first, last):
         @pl.loop(first, last)
@@ -527,15 +531,13 @@
         slot_grads.at[:, slots_at(me), :], bag_grads.at[samples_at(me)], local_sem.at[7]
     )
     own_bags.start()
-    sum_x(0)
+    sum_z(0)
     bags_back(8, 16)
     spread_y(1)
-    sum_y(0)
     bags_back(16, 24)
-    sum_z(0)
+    spread_y(0)
     bags_back(24, EMB)
     spread_cores(1)
-    spread_y(0)
     spread_cores(0)
     settle(1)
     settle(0)
@@ -633,7 +635,9 @@
     )(*operands)
 
 
-def finish_kernel(layer_out, bag_grads, whole, layer_final, bag_final, up, down, held, sums, in_sem, out_sem, sum_sem):
+def finish_kernel(
+    layer_out, bag_grads, whole, layer_final, bag_final, up, down, held, sums_in, sums, in_sem, out_sem, sum_sem,
+):
     pairs = ((layer_out, layer_final), (bag_grads, bag_final))
     rows = [layer_out.shape[0] // 2, bag_grads.shape[0] // 2]
     incoming, outgoing = [], []
@@ -643,13 +647,15 @@
             here = held[n].at[part]
             incoming.append(pltpu.make_async_copy(src.at[part], here, in_sem.at[n, half]))
             outgoing.append(pltpu.make_async_copy(here, dst.at[part], out_sem.at[n, half]))
-    for copy in incoming:
+    sums_copies = [pltpu.make_async_copy(whole.at[kind], sums_in.at[kind], in_sem.at[2, kind]) for kind in range(2)]
+    for copy in sums_copies + incoming:
         copy.start()
     sum_copies = []
     for kind, out in enumerate((up, down)):
+        sums_copies[kind].wait()
         for y in range(YS):
             part = pl.ds(y * 256, 256)
-            sums[kind, part] = whole[kind, part].astype(F32)
+            sums[kind, part] = sums_in[kind, part].astype(F32)
             copy = pltpu.make_async_copy(sums.at[kind, part], out.at[part], sum_sem.at[kind, y])
             copy.start()
             sum_copies.append(copy)
@@ -673,12 +679,13 @@
             jax.ShapeDtypeStruct((SLICE, E), F32),
             jax.ShapeDtypeStruct((SLICE, E), F32),
         ),
-        in_specs=[anywhere, anywhere, pl.BlockSpec(memory_space=pltpu.VMEM)],
+        in_specs=[anywhere] * 3,
         out_specs=(anywhere,) * 4,
         scratch_shapes=[
             [pltpu.VMEM(layer_out.shape, BF16), pltpu.VMEM(bag_grads.shape, BF16)],
+            pltpu.VMEM((2, SLICE, E), BF16),
             pltpu.VMEM((2, SLICE, E), F32),
-            dma((2, 2)),
+            dma((3, 2)),
             dma((2, 2)),
             dma((2, YS)),
         ],

time: 152 us -> 147 us (0.967); the launches traced: 151 us -> 144 us
  Pallas kernels: 150 us -> 144 us
    pallas_call x1, Pallas kernels: 146 us -> 140 us  [whole_layer(): pl.pallas_call(layer_kernel, name='whole_layer', out_shape=(jax.ShapeDtyp...]
where the time goes in v6:
time: 147 us; the launch traced here: 144 us
  Pallas kernels  144 us (98%)
    pallas_call x1, Pallas kernels, whole_layer(): pl.pallas_call(layer_kernel, name='whole_layer', out_shape=(jax.ShapeDtyp...  140 us
    pallas_call x1, Pallas kernels, finish_outputs(): pl.pallas_call(finish_kernel, name='finish_outputs', out_shape=(jax.Shape...  3.35 us

profile of v6, /device:TPU:3, one launch (start us, length us, event | category | flops | bytes accessed | tf_op | source)
XLA Modules:
  0.0 144.5 jit_solution(11160605050813661992)
XLA Ops:
  0.6 140.3 %whole_layer.1 = (bf16[4,512,256]{2,1,0:T(8,128)(2,1)}, bf16[128,16,256]{2,1,0:T(8,128)(2,1)}, bf16[2,1024,256]{2,1,0:T(8,128)(2,1)}) custom-call(s32[16,4,128]{2,1,0:T(4,128)} %bitcast.13, s32[16,128]{1,0:T(8,128)} %bitcast.14, s32[1,512]{1,0:T(1,128)} %bitcast.15, f32[1,256]{1,0:T(1,128)} %bitcast.16, f32[1,256]{1,0:T(1,128)} %bitcast.17, ...), custom_call_target="tpu_custom_call" | custom-call | tf_op jit(solution)/shard_map/whole_layer/pallas_call | solution.py:566
  141.0 3.4 %finish_outputs.1 = (bf16[4,512,256]{2,1,0:T(8,128)(2,1)}, bf16[128,16,256]{2,1,0:T(8,128)(2,1)}, f32[1024,256]{1,0:T(8,128)}, f32[1024,256]{1,0:T(8,128)}) custom-call(bf16[4,512,256]{2,1,0:T(8,128)(2,1)} %get-tuple-element.11.layer_out, bf16[128,16,256]{2,1,0:T(8,128)(2,1)} %get-tuple-element.12.bag_grads, bf16[2,1024,256]{2,1,0:T(8,128)(2,1)} %get-tuple-element.13.whole), custom_call_target="tpu_custom_call" | custom-call | tf_op jit(solution)/shard_map/finish_outputs/pallas_call | solution.py:673

commit v7 on v6

--- a/solution.py
+++ b/solution.py
@@ -21,6 +21,7 @@
 SLOTS = 16
 GROUP_B = 128
 EMB = 32
+STEP = 11
 XS = 4
 YS = 4
 ZS = 4
@@ -86,6 +87,9 @@
     y = lax.rem(me // 2, YS)
     z = me // (2 * YS)
     sibling = me + 1 - 2 * core
+
+    def peer_at(k):
+        return lax.rem(me + lax.rem(k * STEP, EMB), EMB)
 
     def x_at(offset):
         return lax.rem(x + XS + offset, XS)
@@ -183,7 +187,7 @@
 
     @pl.loop(1, EMB)
     def _(k):
-        peer = lax.rem(me + k, EMB)
+        peer = peer_at(k)
         send(
             outgoing.at[samples_at(peer)], slots.at[:, slots_at(me), :], bag_send.at[k], bag_recv.at[k], emb=peer
         ).start()
@@ -212,7 +216,7 @@
 
     @pl.loop(1, EMB)
     def _(k):
-        source = lax.rem(me + EMB - k, EMB)
+        source = lax.rem(me + EMB - lax.rem(k * STEP, EMB), EMB)
         copy = send(
             outgoing.at[samples_at(source)],
             slots.at[:, slots_at(source), :],
@@ -250,7 +254,7 @@
     def forward(group, k):
         chunk = x_at(-k)
 
-        @pl.loop(0, 2)
+        @pl.loop(0, 2, unroll=True)
         def _(t):
             tile = chunk * 2 + t
             here = pl.ds(pl.multiple_of(t * TH, TH), TH)
@@ -473,7 +477,7 @@
         keep(0, tile, dot(rows_t[0], mine) + dot(rows_t[1], theirs))
 
     def chunk_back(k):
-        @pl.loop(0, 2)
+        @pl.loop(0, 2, unroll=True)
         def _(t):
             both_back(k, t)
 
@@ -517,7 +521,7 @@
     def bags_back(first, last):
         @pl.loop(first, last)
         def _(k):
-            peer = lax.rem(me + k, EMB)
+            peer = peer_at(k)
             send(
                 slot_grads.at[:, slots_at(peer), :],
                 bag_grads.at[samples_at(me)],
@@ -544,7 +548,7 @@
 
     @pl.loop(1, EMB)
     def _(k):
-        source = lax.rem(me + EMB - k, EMB)
+        source = lax.rem(me + EMB - lax.rem(k * STEP, EMB), EMB)
         copy = send(
             slot_grads.at[:, slots_at(source), :],
             bag_grads.at[samples_at(source)],

time: 147 us -> 144 us (0.980)
  the two profiles are of different devices: /device:TPU:3 before, /device:TPU:35 now
where the time goes in v7:
time: 144 us
  Pallas kernels  143 us (99%)
    pallas_call x1, Pallas kernels, whole_layer(): pl.pallas_call(layer_kernel, name='whole_layer', out_shape=(jax.ShapeDtyp...  140 us
    pallas_call x1, Pallas kernels, finish_outputs(): pl.pallas_call(finish_kernel, name='finish_outputs', out_shape=(jax.Shape...  3.35 us

profile of v7, /device:TPU:35, one launch (start us, length us, event | category | flops | bytes accessed | tf_op | source)
XLA Modules:
  0.0 144.1 jit_solution(4736546573807887866)
XLA Ops:
  0.6 140.0 %whole_layer.1 = (bf16[4,512,256]{2,1,0:T(8,128)(2,1)}, bf16[128,16,256]{2,1,0:T(8,128)(2,1)}, bf16[2,1024,256]{2,1,0:T(8,128)(2,1)}) custom-call(s32[16,4,128]{2,1,0:T(4,128)} %bitcast.13, s32[16,128]{1,0:T(8,128)} %bitcast.14, s32[1,512]{1,0:T(1,128)} %bitcast.15, f32[1,256]{1,0:T(1,128)} %bitcast.16, f32[1,256]{1,0:T(1,128)} %bitcast.17, ...), custom_call_target="tpu_custom_call" | custom-call | tf_op jit(solution)/shard_map/whole_layer/pallas_call | solution.py:570
  140.6 3.4 %finish_outputs.1 = (bf16[4,512,256]{2,1,0:T(8,128)(2,1)}, bf16[128,16,256]{2,1,0:T(8,128)(2,1)}, f32[1024,256]{1,0:T(8,128)}, f32[1024,256]{1,0:T(8,128)}) custom-call(bf16[4,512,256]{2,1,0:T(8,128)(2,1)} %get-tuple-element.11.layer_out, bf16[128,16,256]{2,1,0:T(8,128)(2,1)} %get-tuple-element.12.bag_grads, bf16[2,1024,256]{2,1,0:T(8,128)(2,1)} %get-tuple-element.13.whole), custom_call_target="tpu_custom_call" | custom-call | tf_op jit(solution)/shard_map/finish_outputs/pallas_call | solution.py:677

commit v8 on v7

--- a/solution.py
+++ b/solution.py
@@ -246,7 +246,7 @@
         rows[0, rows_of(b), :] = (unit * fm_gain[...]).astype(BF16)
         return 0
 
-    lax.fori_loop(0, SAMPLES, embed, 0)
+    lax.fori_loop(0, SAMPLES, embed, 0, unroll=True)
     rows_copy = exchange(rows.at[0], rows.at[1], 0)
     rows_copy.start()
     ff[...] = jnp.zeros_like(ff)
@@ -301,7 +301,7 @@
         grad_rows[0, rows_of(b), :] = finish(total, b, 0, NF)
         return 0
 
-    lax.fori_loop(0, SAMPLES, finish_ff, 0)
+    lax.fori_loop(0, SAMPLES, finish_ff, 0, unroll=True)
     grad_copy = exchange(grad_rows.at[0], grad_rows.at[1], 2)
     grad_copy.start()
 
@@ -513,10 +513,10 @@
         slot_grads[b] = dot(by_slot[...], total.astype(BF16)).astype(BF16)
         return 0
 
-    lax.fori_loop(0, SAMPLES // 2, tail, 0)
+    lax.fori_loop(0, SAMPLES // 2, tail, 0, unroll=True)
     sum_z(1)
     sum_y(0)
-    lax.fori_loop(SAMPLES // 2, SAMPLES, tail, 0)
+    lax.fori_loop(SAMPLES // 2, SAMPLES, tail, 0, unroll=True)
 
     def bags_back(first, last):
         @pl.loop(first, last)
@@ -536,11 +536,9 @@
     )
     own_bags.start()
     sum_z(0)
-    bags_back(8, 16)
+    bags_back(8, EMB)
     spread_y(1)
-    bags_back(16, 24)
     spread_y(0)
-    bags_back(24, EMB)
     spread_cores(1)
     spread_cores(0)
     settle(1)

time: 144 us -> 141 us (0.979)
  the two profiles are of different devices: /device:TPU:35 before, /device:TPU:3 now
where the time goes in v8:
time: 141 us; the launch traced here: 140 us
  Pallas kernels  139 us (99%)
    pallas_call x1, Pallas kernels, whole_layer(): pl.pallas_call(layer_kernel, name='whole_layer', out_shape=(jax.ShapeDtyp...  135 us
    pallas_call x1, Pallas kernels, finish_outputs(): pl.pallas_call(finish_kernel, name='finish_outputs', out_shape=(jax.Shape...  3.35 us

profile of v8, /device:TPU:3, one launch (start us, length us, event | category | flops | bytes accessed | tf_op | source)
XLA Modules:
  0.0 139.5 jit_solution(894523896744161070)
XLA Ops:
  0.6 135.4 %whole_layer.1 = (bf16[4,512,256]{2,1,0:T(8,128)(2,1)}, bf16[128,16,256]{2,1,0:T(8,128)(2,1)}, bf16[2,1024,256]{2,1,0:T(8,128)(2,1)}) custom-call(s32[16,4,128]{2,1,0:T(4,128)} %bitcast.13, s32[16,128]{1,0:T(8,128)} %bitcast.14, s32[1,512]{1,0:T(1,128)} %bitcast.15, f32[1,256]{1,0:T(1,128)} %bitcast.16, f32[1,256]{1,0:T(1,128)} %bitcast.17, ...), custom_call_target="tpu_custom_call" | custom-call | tf_op jit(solution)/shard_map/whole_layer/pallas_call | solution.py:568
  136.0 3.4 %finish_outputs.1 = (bf16[4,512,256]{2,1,0:T(8,128)(2,1)}, bf16[128,16,256]{2,1,0:T(8,128)(2,1)}, f32[1024,256]{1,0:T(8,128)}, f32[1024,256]{1,0:T(8,128)}) custom-call(bf16[4,512,256]{2,1,0:T(8,128)(2,1)} %get-tuple-element.11.layer_out, bf16[128,16,256]{2,1,0:T(8,128)(2,1)} %get-tuple-element.12.bag_grads, bf16[2,1024,256]{2,1,0:T(8,128)(2,1)} %get-tuple-element.13.whole), custom_call_target="tpu_custom_call" | custom-call | tf_op jit(solution)/shard_map/finish_outputs/pallas_call | solution.py:675
